TPU v7x, 256 devices: a whole 4x4x8 slice. The times are simulated.
256 devices in a mesh: dp: 16 (over z_lo, x), expert: 16 (over y, z_hi, core).
Axes of the slice: x: 4, y: 4, z: 8 (z_hi: 2, z_lo: 4; z = z_hi * 4 + z_lo), core: 2. Of those that a mesh axis runs over, the one named last changes fastest.
Arguments:
- tokens: bfloat16 [32768, 2048], P(('dp', 'expert')), may hold values from -24 to 24
- teacher: bfloat16 [32768, 2048], P(('dp', 'expert')), may hold values from -12 to 12
- expert_ids: int32 [32768, 8], P(('dp', 'expert')), may hold values from 0 to 15, all different within a row; in each aligned block of 128 rows (0 to 127, 128 to 255, ...) at most 66 rows name the same one
- route_gates: float32 [32768, 8], P(('dp', 'expert')), may hold values from 0.02 to 0.5
- placement: int32 [16], replicated, may hold values from 0 to 15, as said below
- gate_up_weight: bfloat16 [16, 2048, 768], P('expert'), may hold values from -0.125 to 0.125
- down_weight: bfloat16 [16, 384, 2048], P('expert'), may hold values from -0.3125 to 0.3125
Outputs:
- layer_out: bfloat16 [32768, 2048], P(('dp', 'expert'))
- token_grad: bfloat16 [32768, 2048], P(('dp', 'expert'))
- gate_up_grad: float32 [16, 2048, 768], P('expert', 'dp')
- down_grad: float32 [16, 384, 2048], P('expert', None, 'dp')
Inputs may be any that keep to these rules, and one draw needn't show every extreme that they name: `expert_ids`: each row names 8 different experts. Among the rows of one device no expert is named by more than 66 rows, and in every draw some expert is named by exactly 66 rows of some device. `placement`: A permutation of the positions: the devices along expert form pairs, and each pair exchanges one slot of one device with one slot of the other; all other experts e sit at position e.
All inputs are finite; a program needn't handle non-finite values.
Results may differ from a plain program's by a relative error of at most 0.017.
Values may be sent and summed in bfloat16 or wider, within the bound.
No kernel may reach another device: no remote copies, remote signals or barrier semaphores. Data moves between devices by JAX's collectives and lax.ppermute only.
A program may use at most 128 MiB of HBM per device.

v0:
```python
import functools

import jax
import jax.numpy as jnp
from jax import lax
from jax.experimental import pallas as pl
from jax.experimental.pallas import tpu as pltpu
from jax.sharding import PartitionSpec as P


BF = jnp.bfloat16
F32 = jnp.float32
NY = 4
NX = 4
NZ = 4


def expert_perm(dy, dz, dc):
    out = []
    for y in range(NY):
        for z in range(2):
            for c in range(2):
                src = ((y + dy) % NY) * 4 + (z ^ dz) * 2 + (c ^ dc)
                out.append((src, y * 4 + z * 2 + c))
    return out


def dp_perm(dzl, dx):
    out = []
    for z in range(NZ):
        for x in range(NX):
            src = ((z + dzl) % NZ) * NX + (x + dx) % NX
            out.append((src, z * NX + x))
    return out


def from_expert(value, dy, dz, dc):
    return lax.ppermute(value, "expert", expert_perm(dy, dz, dc))


def from_dp(value, dzl, dx):
    return lax.ppermute(value, "dp", dp_perm(dzl, dx))


def mm(a, b, dims):
    return lax.dot_general(a, b, (dims, ((), ())), preferred_element_type=F32)


def tie(*values):
    return lax.optimization_barrier(values)


def gather_y(start):
    blocks = [start] + [from_expert(start, dy, 0, 0) for dy in (2, 1, 3)]
    return jnp.concatenate([blocks[0], blocks[2], blocks[1], blocks[3]], axis=0)


def scatter_y(blocks, own):
    total = own.astype(F32)
    for dy in (2, 1, 3):
        total = total + from_expert(blocks[dy], -dy, 0, 0).astype(F32)
    return total


def across(value):
    return from_expert(value, 0, 0, 1)


def joined(part, other, rows):
    got = across(other.astype(BF))
    out = []
    for dy in range(NY):
        at = slice(dy * rows, (dy + 1) * rows)
        out.append((part[at].astype(F32) + got[at].astype(F32)).astype(BF))
    return out


LANES = 128


def grad_kernel(x_ref, *refs, first):
    columns, refs = refs[:8], refs[8:]
    sides, refs = refs[:6], refs[6:]
    acc, refs = (None, refs) if first else (refs[0], refs[1:])
    outs, turned = refs[:-1], refs[-1]
    ff = sides[0].shape[1]

    @pl.when((pl.program_id(0) == 0) & (pl.program_id(1) == 0))
    def _():
        for k in range(6):
            turned[k] = sides[k][...].astype(F32).T.astype(BF)

    def product(k, at):
        wide = jnp.concatenate([columns[at][...], columns[at + 1][...]], axis=1)
        return mm(turned[k], wide, ((1,), (0,)))

    parts = [
        product(0, 0) + product(3, 2),
        product(1, 0) + product(4, 2),
        product(2, 4) + product(5, 6),
    ]

    def store(out, *lead):
        for k in range(3):
            rows = slice(k * ff, (k + 1) * ff)
            for z in range(2):
                value = parts[k][:, z * LANES : (z + 1) * LANES]
                if acc is not None:
                    value = value + acc[0, z, rows, :]
                out[(*lead, z, rows, slice(None))] = value.astype(out.dtype)

    if first:
        store(outs[0], 0)
    else:
        for k in range(NX):

            @pl.when(pl.program_id(0) == k)
            def _(k=k):
                store(outs[k])


def weight_grads(row_blocks, res, sides, acc):
    count, features = row_blocks[0].shape
    ff = sides[0].shape[1]
    x_at = (lax.axis_index("dp") % NX).astype(jnp.int32).reshape(1)

    def column(second):
        return pl.BlockSpec(
            (count, LANES),
            lambda i, j, x: (0, (2 * j + second) * NX + (x[0] + i) % NX),
        )

    args, specs = [], []
    for array in (*row_blocks, *res):
        args += [array, array]
        specs += [column(0), column(1)]
    args += sides
    specs += [pl.BlockSpec((count, ff), lambda i, j, x: (0, 0))] * 6
    whole = (NX, NZ, 3 * ff, LANES)
    acc_spec = pl.BlockSpec((1, 2, 3 * ff, LANES), lambda i, j, x: (i, j, 0, 0))
    if acc is None:
        out_specs = [acc_spec]
        out_shape = [jax.ShapeDtypeStruct(whole, F32)]
    else:
        args.append(acc)
        specs.append(acc_spec)

        def block_of(k):
            def index(i, j, x):
                return (jnp.where(i == k, j, jnp.where(i < k, 0, 1)), 0, 0)

            return pl.BlockSpec((2, 3 * ff, LANES), index)

        out_specs = [block_of(k) for k in range(NX)]
        out_shape = [jax.ShapeDtypeStruct(whole[1:], BF)] * NX
    return pl.pallas_call(
        functools.partial(grad_kernel, first=acc is None),
        grid_spec=pltpu.PrefetchScalarGridSpec(
            num_scalar_prefetch=1,
            grid=(NX, NZ // 2),
            in_specs=specs,
            out_specs=out_specs,
            scratch_shapes=[pltpu.VMEM((6, ff, count), BF)],
        ),
        out_shape=out_shape,
        name="weight_grads",
        cost_estimate=pl.CostEstimate(
            flops=12 * count * features * ff,
            transcendentals=0,
            bytes_accessed=8 * count * features + 24 * features * ff,
        ),
    )(x_at, *args)


def x_stage(blocks):
    return [from_dp(blocks[dx], 0, -dx) for dx in (2, 1, 3)]


def z_stage(total):
    z_at = lax.axis_index("dp") // NX
    result = lax.dynamic_index_in_dim(total, z_at, 0, keepdims=False)
    rounded = total.astype(BF)
    for dzl in (2, 1, 3):
        part = lax.dynamic_index_in_dim(rounded, (z_at + dzl) % NZ, 0, keepdims=False)
        result = result + from_dp(part, -dzl, 0).astype(F32)
    return result


def shards(tokens, teacher, expert_ids, route_gates, placement, gate_up_weight, down_weight):
    rows = tokens.shape[0]
    w_gu = gate_up_weight[0]
    w_dn = down_weight[0]
    ff = w_dn.shape[0]
    count = lax.axis_size("expert")
    here = lax.axis_index("expert")
    y_at, z_at, c_at = here // 4, (here // 2) % 2, here % 2

    table = jnp.arange(count, dtype=jnp.int32)
    chosen = expert_ids[:, :, None] == table
    position = jnp.sum(jnp.where(chosen, placement, 0), axis=2)
    gate_of = jnp.sum(
        jnp.where(table[:, None, None] == position[None], route_gates[None], 0.0), axis=2
    )

    far_rows = from_expert(tokens, 0, 1, 0)
    near = gather_y(tokens)
    gate_in = lax.all_to_all(gate_of, "expert", split_axis=0, concat_axis=0, tiled=True)
    near, far_rows, gate_in = tie(near, far_rows, gate_in)

    def gates(dz, dc):
        out = []
        for dy in range(NY):
            src = ((y_at + dy) % NY) * 4 + (z_at ^ dz) * 2 + (c_at ^ dc)
            out.append(jnp.sum(jnp.where(table[:, None] == src, gate_in, 0.0), axis=0))
        return jnp.concatenate(out)[:, None]

    def forward(row_block, gate):
        pre = mm(row_block, w_gu, ((1,), (0,)))
        g, u = pre[:, :ff], pre[:, ff:]
        s = jax.nn.sigmoid(g)
        hidden = (gate * (g * s) * u).astype(BF)
        return pre, hidden, mm(hidden, w_dn, ((1,), (0,)))

    def backward(res_block, saved):
        pre, gate = saved
        g, u = pre[:, :ff], pre[:, ff:]
        s = jax.nn.sigmoid(g)
        grad = gate * mm(res_block, w_dn, ((1,), (1,)))
        at_gate = (grad * u * (s * (1.0 + g * (1.0 - s)))).astype(BF)
        at_up = (grad * (g * s)).astype(BF)
        mixed = jnp.concatenate([at_gate, at_up], axis=1)
        return at_gate, at_up, mm(mixed, w_gu, ((1,), (1,)))

    gate = [[gates(dz, dc) for dc in (0, 1)] for dz in (0, 1)]
    saved = [[None, None], [None, None]]
    hidden = [[None, None], [None, None]]

    far = gather_y(far_rows)
    row_blocks = [[near, across(near)], None]
    both = [None, None]
    for dz in (0, 1):
        if dz == 1:
            far, near_own = tie(far, both[0][0])
            row_blocks[1] = [far, across(far)]
        outs = [None, None]
        for dc in (1, 0):
            pre, hidden[dz][dc], outs[dc] = forward(row_blocks[dz][dc], gate[dz][dc])
            saved[dz][dc] = (pre, gate[dz][dc])
        both[dz] = joined(outs[0], outs[1], rows)
    far_sum = scatter_y(both[1], both[1][0])
    near_sum = scatter_y(both[0], near_own)
    layer_sum = near_sum + from_expert(far_sum.astype(BF), 0, 1, 0).astype(F32)
    layer_out = layer_sum.astype(BF)
    residual = (layer_sum - teacher.astype(F32)).astype(BF)

    far_res = from_expert(residual, 0, 1, 0)
    near_res = gather_y(residual)
    near_res, far_res = tie(near_res, far_res)
    far_res = gather_y(far_res)
    res = [near_res, across(near_res)]
    near_back = [backward(res[dc], saved[0][dc]) for dc in (0, 1)]
    near_both = joined(near_back[0][2], near_back[1][2], rows)
    near_sum = scatter_y(near_both, near_both[0])

    def sides(dz, back):
        out = []
        for dc in (0, 1):
            out += [back[dc][0], back[dc][1], hidden[dz][dc]]
        return out

    (term,) = weight_grads(row_blocks[0], res, sides(0, near_back), None)

    res = [far_res, across(far_res)]
    back = [backward(res[dc], saved[1][dc]) for dc in (0, 1)]
    blocks = weight_grads(row_blocks[1], res, sides(1, back), term)
    got = x_stage(blocks)
    far_both = joined(back[0][2], back[1][2], rows)
    far_sum = scatter_y(far_both, far_both[0]).astype(BF)
    crossed = from_expert(far_sum, 0, 1, 0)

    total = blocks[0].astype(F32)
    for part in got:
        total = total + part.astype(F32)
    share = z_stage(total)
    token_sum = near_sum + crossed.astype(F32)
    split = 2 * ff
    return (layer_out, token_sum.astype(BF), share[:split].T[None], share[split:][None])


def solution(mesh):
    in_specs = (
        P(("dp", "expert"), None),
        P(("dp", "expert"), None),
        P(("dp", "expert"), None),
        P(("dp", "expert"), None),
        P(),
        P("expert", None, None),
        P("expert", None, None),
    )
    out_specs = (
        P(("dp", "expert"), None),
        P(("dp", "expert"), None),
        P("expert", "dp", None),
        P("expert", None, "dp"),
    )

    return jax.shard_map(shards, mesh=mesh, in_specs=in_specs, out_specs=out_specs, check_vma=False)
```

profile of v0, /device:TPU:2, one launch (start us, length us, event | category | flops | bytes accessed | tf_op | source)
XLA Modules:
  0.0 377.1 jit_solution(9571653972915951628)
XLA Ops:
  5.3 7.2 %collective-permute-start.3 = (bf16[128,2048]{1,0:T(8,128)(2,1)}, bf16[128,2048]{1,0:T(8,128)(2,1)}, u32[]{:S(2)}, u32[]{:S(2)}) collective-permute-start(bf16[128,2048]{1,0:T(8,128)(2,1)} %param.7), channel_id=1, source_target_pairs={{2,0},{3,1},{0,2},{1,3},{6,4},{7,5},{4,6},{5,7},{10,8},{11,9},{8,1... | collective-permute-start | bytes 1572872 | tf_op jit(solution)/shard_map/ppermute | solution.py:38
  14.6 3.6 all-to-all-start
  18.3 8.3 %collective-permute-done = bf16[128,2048]{1,0:T(8,128)(2,1)} collective-permute-done((bf16[128,2048]{1,0:T(8,128)(2,1)}, bf16[128,2048]{1,0:T(8,128)(2,1)}, u32[]{:S(2)}, u32[]{:S(2)}) %collective-permute-start) | collective-permute-done | bytes 524320 | tf_op jit(solution)/shard_map/ppermute | solution.py:38
  26.6 3.7 collective-permute-done.2
  34.0 3.9 %collective-permute-done.7.refs_2_.refs_3_ = bf16[512,2048]{1,0:T(8,128)(2,1)} collective-permute-done((bf16[512,2048]{1,0:T(8,128)(2,1)}, bf16[512,2048]{1,0:T(8,128)(2,1)}, u32[]{:S(2)}, u32[]{:S(2)}) %collective-permute-start.7) | collective-permute-done | bytes 2097184 | tf_op jit(solution)/shard_map/ppermute | solution.py:38
  49.8 9.4 %collective-permute-done.4 = bf16[128,2048]{1,0:T(8,128)(2,1)S(1)} collective-permute-done((bf16[128,2048]{1,0:T(8,128)(2,1)}, bf16[128,2048]{1,0:T(8,128)(2,1)S(1)}, u32[]{:S(2)}, u32[]{:S(2)}) %collective-permute-start.4) | collective-permute-done | bytes 524320 | tf_op jit(solution)/shard_map/ppermute | solution.py:38
  61.5 10.3 %collective-permute-done.6 = bf16[128,2048]{1,0:T(8,128)(2,1)S(1)} collective-permute-done((bf16[128,2048]{1,0:T(8,128)(2,1)}, bf16[128,2048]{1,0:T(8,128)(2,1)S(1)}, u32[]{:S(2)}, u32[]{:S(2)}) %collective-permute-start.6) | collective-permute-done | bytes 524320 | tf_op jit(solution)/shard_map/ppermute | solution.py:38
  73.9 4.1 %collective-permute-done.12.refs_2_.refs_3_ = bf16[512,2048]{1,0:T(8,128)(2,1)S(1)} collective-permute-done((bf16[512,2048]{1,0:T(8,128)(2,1)S(1)}, bf16[512,2048]{1,0:T(8,128)(2,1)S(1)}, u32[]{:S(2)}, u32[]{:S(2)}) %collective-permute-start.12) | collective-permute-done | bytes 2097184 | tf_op jit(solution)/shard_map/ppermute | solution.py:38
  94.5 9.1 %collective-permute-done.14 = bf16[128,2048]{1,0:T(8,128)(2,1)S(1)} collective-permute-done((bf16[128,2048]{1,0:T(8,128)(2,1)S(1)}, bf16[128,2048]{1,0:T(8,128)(2,1)S(1)}, u32[]{:S(2)}, u32[]{:S(2)}) %collective-permute-start.14) | collective-permute-done | bytes 524320 | tf_op jit(solution)/shard_map/ppermute | solution.py:38
  104.2 9.8 %collective-permute-done.15 = bf16[128,2048]{1,0:T(8,128)(2,1)S(1)} collective-permute-done((bf16[128,2048]{1,0:T(8,128)(2,1)S(1)}, bf16[128,2048]{1,0:T(8,128)(2,1)S(1)}, u32[]{:S(2)}, u32[]{:S(2)}) %collective-permute-start.15) | collective-permute-done | bytes 524320 | tf_op jit(solution)/shard_map/ppermute | solution.py:38
  114.4 10.3 %collective-permute-start.17 = (bf16[128,2048]{1,0:T(8,128)(2,1)S(1)}, bf16[128,2048]{1,0:T(8,128)(2,1)S(1)}, u32[]{:S(2)}, u32[]{:S(2)}) collective-permute-start(bf16[128,2048]{1,0:T(8,128)(2,1)S(1)} %add_convert_fusion.2), channel_id=1, source_target_pairs={{2,0},{3,1},{0,2},{1,3},{6,4},{7,5},{4,6},{5,7},{10,8},{11,9},{8,1... | collective-permute-start | bytes 1572872 | tf_op jit(solution)/shard_map/ppermute | solution.py:38
  125.9 10.5 %collective-permute-done.9 = bf16[128,2048]{1,0:T(8,128)(2,1)S(1)} collective-permute-done((bf16[128,2048]{1,0:T(8,128)(2,1)S(1)}, bf16[128,2048]{1,0:T(8,128)(2,1)S(1)}, u32[]{:S(2)}, u32[]{:S(2)}) %collective-permute-start.9) | collective-permute-done | bytes 524320 | tf_op jit(solution)/shard_map/ppermute | solution.py:38
  141.5 15.6 %collective-permute-start.21 = (bf16[128,2048]{1,0:T(8,128)(2,1)S(1)}, bf16[128,2048]{1,0:T(8,128)(2,1)S(1)}, u32[]{:S(2)}, u32[]{:S(2)}) collective-permute-start(bf16[128,2048]{1,0:T(8,128)(2,1)S(1)} %get-tuple-element.61), channel_id=1, source_target_pairs={{2,0},{3,1},{0,2},{1,3},{6,4},{7,5},{4,6},{5,7},{10,8},{11,9},{8,1... | collective-permute-start | bytes 1572872 | tf_op jit(solution)/shard_map/ppermute | solution.py:38
  157.1 7.8 %collective-permute-done.20 = bf16[128,2048]{1,0:T(8,128)(2,1)S(1)} collective-permute-done((bf16[128,2048]{1,0:T(8,128)(2,1)S(1)}, bf16[128,2048]{1,0:T(8,128)(2,1)S(1)}, u32[]{:S(2)}, u32[]{:S(2)}) %collective-permute-start.20) | collective-permute-done | bytes 524320 | tf_op jit(solution)/shard_map/ppermute | solution.py:38
  166.5 8.0 %collective-permute-done.21 = bf16[128,2048]{1,0:T(8,128)(2,1)S(1)} collective-permute-done((bf16[128,2048]{1,0:T(8,128)(2,1)S(1)}, bf16[128,2048]{1,0:T(8,128)(2,1)S(1)}, u32[]{:S(2)}, u32[]{:S(2)}) %collective-permute-start.21) | collective-permute-done | bytes 524320 | tf_op jit(solution)/shard_map/ppermute | solution.py:38
  179.8 6.1 %collective-permute-done.27 = bf16[128,2048]{1,0:T(8,128)(2,1)S(1)} collective-permute-done((bf16[128,2048]{1,0:T(8,128)(2,1)S(1)}, bf16[128,2048]{1,0:T(8,128)(2,1)S(1)}, u32[]{:S(2)}, u32[]{:S(2)}) %collective-permute-start.27) | collective-permute-done | bytes 524320 | tf_op jit(solution)/shard_map/ppermute | solution.py:38
  188.5 4.6 %collective-permute-done.29 = bf16[128,2048]{1,0:T(8,128)(2,1)S(1)} collective-permute-done((bf16[128,2048]{1,0:T(8,128)(2,1)S(1)}, bf16[128,2048]{1,0:T(8,128)(2,1)S(1)}, u32[]{:S(2)}, u32[]{:S(2)}) %collective-permute-start.29) | collective-permute-done | bytes 524320 | tf_op jit(solution)/shard_map/ppermute | solution.py:38
  194.4 5.0 %multiply_convert_fusion.7 = (bf16[512,384]{1,0:T(8,128)(2,1)}, bf16[512,384]{1,0:T(8,128)(2,1)}) fusion(f32[512,768]{1,0:T(8,128)} %copy-done.15, bf16[512,2048]{1,0:T(8,128)(2,1)} %pad_maximum_fusion.2.refs_4_.refs_5_, bf16[1,384,2048]{2,1,0:T(8,128)(2,1)} %param.13, f32[512]{0:T(512)S(1)} %get-tuple-element.74), kind=kOutput, calls=%fused_computation.98 | convolution fusion | flops 808058880 | bytes 6031360 | tf_op jit(solution)/shard_map/dot_general | solution.py:46
  199.4 4.1 %multiply_convert_fusion.3 = (bf16[512,384]{1,0:T(8,128)(2,1)}, bf16[512,384]{1,0:T(8,128)(2,1)}) fusion(f32[512,768]{1,0:T(8,128)S(1)} %copy-done.18, bf16[512,2048]{1,0:T(8,128)(2,1)} %constant_dynamic-update-slice_fusion.refs_4_.refs_5_, bf16[1,384,2048]{2,1,0:T(8,128)(2,1)S(1)} %copy-done.5, f32[512]{0:T(512)S(1)} %get-tuple-element.76), kind=kOutput, calls=%fused_computation.94 | convolution fusion | flops 808058880 | bytes 6031360 | tf_op jit(solution)/shard_map/dot_general | solution.py:46
  203.5 4.0 %multiply_convert_fusion.5 = (bf16[512,384]{1,0:T(8,128)(2,1)}, bf16[512,384]{1,0:T(8,128)(2,1)}) fusion(f32[512,768]{1,0:T(8,128)S(1)} %copy-done.14, bf16[512,2048]{1,0:T(8,128)(2,1)} %collective-permute-done.22.refs_6_.refs_7_, bf16[1,384,2048]{2,1,0:T(8,128)(2,1)S(1)} %copy-done.5, f32[512]{0:T(512)S(1)} %get-tuple-element.75), kind=kOutput, calls=%fused_computation.96 | convolution fusion | flops 808058880 | bytes 6031360 | tf_op jit(solution)/shard_map/dot_general | solution.py:46
  207.5 13.2 %weight_grads.2.refs_14_ = f32[4,4,1152,128]{3,2,1,0:T(8,128)} custom-call(s32[1]{0:T(128)} %bitcast.5.x_ref, bf16[512,2048]{1,0:T(8,128)(2,1)} %pad_maximum_fusion.refs_0_.refs_1_, bf16[512,2048]{1,0:T(8,128)(2,1)} %pad_maximum_fusion.refs_0_.refs_1_, bf16[512,2048]{1,0:T(8,128)(2,1)} %collective-permute-done.7.refs_2_.refs_3_, ...), custom_call_target="tpu_custom_call" | custom-call | flops 4831838208 | bytes 27262976 | tf_op jit(solution)/shard_map/weight_grads/pallas_call | solution.py:156
  220.7 3.9 %multiply_convert_fusion.1 = (bf16[512,384]{1,0:T(8,128)(2,1)S(1)}, bf16[512,384]{1,0:T(8,128)(2,1)S(1)}) fusion(f32[512,768]{1,0:T(8,128)} %copy-done.16, bf16[512,2048]{1,0:T(8,128)(2,1)} %collective-permute-done.30.refs_6_.refs_7_, bf16[1,384,2048]{2,1,0:T(8,128)(2,1)} %param.13, f32[512]{0:T(512)S(1)} %get-tuple-element.77), kind=kOutput, calls=%fused_computation.92 | convolution fusion | flops 808058880 | bytes 6031360 | tf_op jit(solution)/shard_map/dot_general | solution.py:46
  227.8 15.4 %weight_grads.3 = (bf16[4,1152,128]{2,1,0:T(8,128)(2,1)}, bf16[4,1152,128]{2,1,0:T(8,128)(2,1)}, bf16[4,1152,128]{2,1,0:T(8,128)(2,1)}, bf16[4,1152,128]{2,1,0:T(8,128)(2,1)}) custom-call(s32[1]{0:T(128)} %bitcast.5.x_ref, bf16[512,2048]{1,0:T(8,128)(2,1)} %copy-done.2, bf16[512,2048]{1,0:T(8,128)(2,1)} %copy-done.2, bf16[512,2048]{1,0:T(8,128)(2,1)} %copy-done.3, ...), custom_call_target="tpu_custom_call" | custom-call | flops 4831838208 | bytes 27262976 | tf_op jit(solution)/shard_map/weight_grads/pallas_call | solution.py:156
  254.8 19.1 %collective-permute-done.36 = bf16[4,1152,128]{2,1,0:T(8,128)(2,1)S(1)} collective-permute-done((bf16[4,1152,128]{2,1,0:T(8,128)(2,1)}, bf16[4,1152,128]{2,1,0:T(8,128)(2,1)S(1)}, u32[]{:S(2)}, u32[]{:S(2)}) %collective-permute-start.36) | collective-permute-done | bytes 1179680 | tf_op jit(solution)/shard_map/ppermute | solution.py:42
  273.9 24.7 %collective-permute-done.37 = bf16[4,1152,128]{2,1,0:T(8,128)(2,1)S(1)} collective-permute-done((bf16[4,1152,128]{2,1,0:T(8,128)(2,1)}, bf16[4,1152,128]{2,1,0:T(8,128)(2,1)S(1)}, u32[]{:S(2)}, u32[]{:S(2)}) %collective-permute-start.37) | collective-permute-done | bytes 1179680 | tf_op jit(solution)/shard_map/ppermute | solution.py:42
  299.3 13.8 %collective-permute-start.39 = (bf16[1152,128]{1,0:T(8,128)(2,1)S(1)}, bf16[1152,128]{1,0:T(8,128)(2,1)S(1)}, u32[]{:S(2)}, u32[]{:S(2)}) collective-permute-start(bf16[1152,128]{1,0:T(8,128)(2,1)S(1)} %get-tuple-element.71), channel_id=1, source_target_pairs={{128,0},{144,16},{160,32},{176,48},{192,64},{208,80},{224,96},{240... | collective-permute-start | bytes 884744 | tf_op jit(solution)/shard_map/ppermute | solution.py:42
  319.0 11.1 %collective-permute-done.32 = bf16[128,2048]{1,0:T(8,128)(2,1)S(1)} collective-permute-done((bf16[128,2048]{1,0:T(8,128)(2,1)S(1)}, bf16[128,2048]{1,0:T(8,128)(2,1)S(1)}, u32[]{:S(2)}, u32[]{:S(2)}) %collective-permute-start.32) | collective-permute-done | bytes 524320 | tf_op jit(solution)/shard_map/ppermute | solution.py:38
  330.1 3.8 %collective-permute-start.41 = (bf16[1152,128]{1,0:T(8,128)(2,1)S(1)}, bf16[1152,128]{1,0:T(8,128)(2,1)S(1)}, u32[]{:S(2)}, u32[]{:S(2)}) collective-permute-start(bf16[1152,128]{1,0:T(8,128)(2,1)S(1)} %get-tuple-element.72), channel_id=1, source_target_pairs={{64,0},{80,16},{96,32},{112,48},{128,64},{144,80},{160,96},{176,11... | collective-permute-start | bytes 884744 | tf_op jit(solution)/shard_map/ppermute | solution.py:42
  333.9 6.1 %collective-permute-done.33 = bf16[128,2048]{1,0:T(8,128)(2,1)S(1)} collective-permute-done((bf16[128,2048]{1,0:T(8,128)(2,1)S(1)}, bf16[128,2048]{1,0:T(8,128)(2,1)S(1)}, u32[]{:S(2)}, u32[]{:S(2)}) %collective-permute-start.33) | collective-permute-done | bytes 524320 | tf_op jit(solution)/shard_map/ppermute | solution.py:38
  345.1 4.6 %collective-permute-start.35 = (bf16[128,2048]{1,0:T(8,128)(2,1)}, bf16[128,2048]{1,0:T(8,128)(2,1)}, u32[]{:S(2)}, u32[]{:S(2)}) collective-permute-start(bf16[128,2048]{1,0:T(8,128)(2,1)} %add_convert_fusion.1), channel_id=1, source_target_pairs={{2,0},{3,1},{0,2},{1,3},{6,4},{7,5},{4,6},{5,7},{10,8},{11,9},{8,1... | collective-permute-start | bytes 1572872 | tf_op jit(solution)/shard_map/ppermute | solution.py:38
  356.7 10.2 %collective-permute-done.25 = bf16[128,2048]{1,0:T(8,128)(2,1)} collective-permute-done((bf16[128,2048]{1,0:T(8,128)(2,1)}, bf16[128,2048]{1,0:T(8,128)(2,1)}, u32[]{:S(2)}, u32[]{:S(2)}) %collective-permute-start.25) | collective-permute-done | bytes 524320 | tf_op jit(solution)/shard_map/ppermute | solution.py:38
  366.9 6.8 %collective-permute-done.35 = bf16[128,2048]{1,0:T(8,128)(2,1)} collective-permute-done((bf16[128,2048]{1,0:T(8,128)(2,1)}, bf16[128,2048]{1,0:T(8,128)(2,1)}, u32[]{:S(2)}, u32[]{:S(2)}) %collective-permute-start.35) | collective-permute-done | bytes 524320 | tf_op jit(solution)/shard_map/ppermute | solution.py:38
  (174 shorter events, 97.3 us)
Async XLA Ops:
  0.6 25.9 %collective-permute-start = (bf16[128,2048]{1,0:T(8,128)(2,1)}, bf16[128,2048]{1,0:T(8,128)(2,1)}, u32[]{:S(2)}, u32[]{:S(2)}) collective-permute-start(bf16[128,2048]{1,0:T(8,128)(2,1)} %param.7), channel_id=1, source_target_pairs={{4,0},{5,1},{6,2},{7,3},{8,4},{9,5},{10,6},{11,7},{12,8},{13,9},{1... | collective-permute-start | bytes 1572872 | tf_op jit(solution)/shard_map/ppermute | solution.py:38
  3.7 22.8 %collective-permute-start.1 = (bf16[128,2048]{1,0:T(8,128)(2,1)}, bf16[128,2048]{1,0:T(8,128)(2,1)}, u32[]{:S(2)}, u32[]{:S(2)}) collective-permute-start(bf16[128,2048]{1,0:T(8,128)(2,1)} %param.7), channel_id=1, source_target_pairs={{8,0},{9,1},{10,2},{11,3},{12,4},{13,5},{14,6},{15,7},{0,8},{1,9},... | collective-permute-start | bytes 1572872 | tf_op jit(solution)/shard_map/ppermute | solution.py:38
  4.4 25.9 %collective-permute-start.2 = (bf16[128,2048]{1,0:T(8,128)(2,1)}, bf16[128,2048]{1,0:T(8,128)(2,1)}, u32[]{:S(2)}, u32[]{:S(2)}) collective-permute-start(bf16[128,2048]{1,0:T(8,128)(2,1)} %param.7), channel_id=1, source_target_pairs={{12,0},{13,1},{14,2},{15,3},{0,4},{1,5},{2,6},{3,7},{4,8},{5,9},{6... | collective-permute-start | bytes 1572872 | tf_op jit(solution)/shard_map/ppermute | solution.py:38
  5.3 28.0 %collective-permute-start.3 = (bf16[128,2048]{1,0:T(8,128)(2,1)}, bf16[128,2048]{1,0:T(8,128)(2,1)}, u32[]{:S(2)}, u32[]{:S(2)}) collective-permute-start(bf16[128,2048]{1,0:T(8,128)(2,1)} %param.7), channel_id=1, source_target_pairs={{2,0},{3,1},{0,2},{1,3},{6,4},{7,5},{4,6},{5,7},{10,8},{11,9},{8,1... | collective-permute-start | bytes 1572872 | tf_op jit(solution)/shard_map/ppermute | solution.py:38
  14.6 18.7 %all-to-all-start = ((f32[16,1,128]{2,1,0:T(1,128)}), f32[16,1,128]{2,1,0:T(1,128)S(1)}, u32[]{:S(2)}, u32[]{:S(2)}) async-start(f32[16,1,128]{2,1,0:T(1,128)} %bitcast.1), calls=%async_computation | async-start | bytes 16384 | tf_op jit(solution)/shard_map/all_to_all | solution.py:207
  44.1 29.0 %collective-permute-start.8 = (bf16[512,2048]{1,0:T(8,128)(2,1)S(1)}, bf16[512,2048]{1,0:T(8,128)(2,1)S(1)}, u32[]{:S(2)}, u32[]{:S(2)}) collective-permute-start(bf16[512,2048]{1,0:T(8,128)(2,1)S(1)} %convolution_convert_fusion.1), channel_id=1, source_target_pairs={{1,0},{0,1},{3,2},{2,3},{5,4},{4,5},{7,6},{6,7},{9,8},{8,9},{11,10... | collective-permute-start | bytes 6291464 | tf_op jit(solution)/shard_map/ppermute | solution.py:38
  45.5 26.2 %collective-permute-start.6 = (bf16[128,2048]{1,0:T(8,128)(2,1)}, bf16[128,2048]{1,0:T(8,128)(2,1)S(1)}, u32[]{:S(2)}, u32[]{:S(2)}) collective-permute-start(bf16[128,2048]{1,0:T(8,128)(2,1)} %collective-permute-done.3), channel_id=1, source_target_pairs={{12,0},{13,1},{14,2},{15,3},{0,4},{1,5},{2,6},{3,7},{4,8},{5,9},{6... | collective-permute-start | bytes 1572872 | tf_op jit(solution)/shard_map/ppermute | solution.py:38
  87.8 26.2 %collective-permute-start.15 = (bf16[128,2048]{1,0:T(8,128)(2,1)S(1)}, bf16[128,2048]{1,0:T(8,128)(2,1)S(1)}, u32[]{:S(2)}, u32[]{:S(2)}) collective-permute-start(bf16[128,2048]{1,0:T(8,128)(2,1)S(1)} %get-tuple-element.60), channel_id=1, source_target_pairs={{12,0},{13,1},{14,2},{15,3},{0,4},{1,5},{2,6},{3,7},{4,8},{5,9},{6... | collective-permute-start | bytes 1572872 | tf_op jit(solution)/shard_map/ppermute | solution.py:38
  88.9 25.1 %collective-permute-start.16 = (bf16[128,2048]{1,0:T(8,128)(2,1)S(1)}, bf16[128,2048]{1,0:T(8,128)(2,1)S(1)}, u32[]{:S(2)}, u32[]{:S(2)}) collective-permute-start(bf16[128,2048]{1,0:T(8,128)(2,1)S(1)} %get-tuple-element.59), channel_id=1, source_target_pairs={{4,0},{5,1},{6,2},{7,3},{8,4},{9,5},{10,6},{11,7},{12,8},{13,9},{1... | collective-permute-start | bytes 1572872 | tf_op jit(solution)/shard_map/ppermute | solution.py:38
  91.3 34.7 %collective-permute-start.10 = (bf16[128,2048]{1,0:T(8,128)(2,1)S(1)}, bf16[128,2048]{1,0:T(8,128)(2,1)S(1)}, u32[]{:S(2)}, u32[]{:S(2)}) collective-permute-start(bf16[128,2048]{1,0:T(8,128)(2,1)S(1)} %get-tuple-element.56), channel_id=1, source_target_pairs={{12,0},{13,1},{14,2},{15,3},{0,4},{1,5},{2,6},{3,7},{4,8},{5,9},{6... | collective-permute-start | bytes 1572872 | tf_op jit(solution)/shard_map/ppermute | solution.py:38
  91.3 34.7 %collective-permute-start.11 = (bf16[128,2048]{1,0:T(8,128)(2,1)S(1)}, bf16[128,2048]{1,0:T(8,128)(2,1)S(1)}, u32[]{:S(2)}, u32[]{:S(2)}) collective-permute-start(bf16[128,2048]{1,0:T(8,128)(2,1)S(1)} %get-tuple-element.55), channel_id=1, source_target_pairs={{4,0},{5,1},{6,2},{7,3},{8,4},{9,5},{10,6},{11,7},{12,8},{13,9},{1... | collective-permute-start | bytes 1572872 | tf_op jit(solution)/shard_map/ppermute | solution.py:38
  103.5 32.9 %collective-permute-start.9 = (bf16[128,2048]{1,0:T(8,128)(2,1)S(1)}, bf16[128,2048]{1,0:T(8,128)(2,1)S(1)}, u32[]{:S(2)}, u32[]{:S(2)}) collective-permute-start(bf16[128,2048]{1,0:T(8,128)(2,1)S(1)} %get-tuple-element.54), channel_id=1, source_target_pairs={{8,0},{9,1},{10,2},{11,3},{12,4},{13,5},{14,6},{15,7},{0,8},{1,9},... | collective-permute-start | bytes 1572872 | tf_op jit(solution)/shard_map/ppermute | solution.py:38
  114.4 23.2 %collective-permute-start.17 = (bf16[128,2048]{1,0:T(8,128)(2,1)S(1)}, bf16[128,2048]{1,0:T(8,128)(2,1)S(1)}, u32[]{:S(2)}, u32[]{:S(2)}) collective-permute-start(bf16[128,2048]{1,0:T(8,128)(2,1)S(1)} %add_convert_fusion.2), channel_id=1, source_target_pairs={{2,0},{3,1},{0,2},{1,3},{6,4},{7,5},{4,6},{5,7},{10,8},{11,9},{8,1... | collective-permute-start | bytes 1572872 | tf_op jit(solution)/shard_map/ppermute | solution.py:38
  139.0 18.1 %collective-permute-start.18 = (bf16[128,2048]{1,0:T(8,128)(2,1)S(1)}, bf16[128,2048]{1,0:T(8,128)(2,1)S(1)}, u32[]{:S(2)}, u32[]{:S(2)}) collective-permute-start(bf16[128,2048]{1,0:T(8,128)(2,1)S(1)} %get-tuple-element.61), channel_id=1, source_target_pairs={{4,0},{5,1},{6,2},{7,3},{8,4},{9,5},{10,6},{11,7},{12,8},{13,9},{1... | collective-permute-start | bytes 1572872 | tf_op jit(solution)/shard_map/ppermute | solution.py:38
  139.6 17.4 %collective-permute-start.19 = (bf16[128,2048]{1,0:T(8,128)(2,1)S(1)}, bf16[128,2048]{1,0:T(8,128)(2,1)S(1)}, u32[]{:S(2)}, u32[]{:S(2)}) collective-permute-start(bf16[128,2048]{1,0:T(8,128)(2,1)S(1)} %get-tuple-element.61), channel_id=1, source_target_pairs={{8,0},{9,1},{10,2},{11,3},{12,4},{13,5},{14,6},{15,7},{0,8},{1,9},... | collective-permute-start | bytes 1572872 | tf_op jit(solution)/shard_map/ppermute | solution.py:38
  140.7 24.2 %collective-permute-start.20 = (bf16[128,2048]{1,0:T(8,128)(2,1)S(1)}, bf16[128,2048]{1,0:T(8,128)(2,1)S(1)}, u32[]{:S(2)}, u32[]{:S(2)}) collective-permute-start(bf16[128,2048]{1,0:T(8,128)(2,1)S(1)} %get-tuple-element.61), channel_id=1, source_target_pairs={{12,0},{13,1},{14,2},{15,3},{0,4},{1,5},{2,6},{3,7},{4,8},{5,9},{6... | collective-permute-start | bytes 1572872 | tf_op jit(solution)/shard_map/ppermute | solution.py:38
  141.5 33.0 %collective-permute-start.21 = (bf16[128,2048]{1,0:T(8,128)(2,1)S(1)}, bf16[128,2048]{1,0:T(8,128)(2,1)S(1)}, u32[]{:S(2)}, u32[]{:S(2)}) collective-permute-start(bf16[128,2048]{1,0:T(8,128)(2,1)S(1)} %get-tuple-element.61), channel_id=1, source_target_pairs={{2,0},{3,1},{0,2},{1,3},{6,4},{7,5},{4,6},{5,7},{10,8},{11,9},{8,1... | collective-permute-start | bytes 1572872 | tf_op jit(solution)/shard_map/ppermute | solution.py:38
  179.0 24.5 %collective-permute-start.22 = (bf16[512,2048]{1,0:T(8,128)(2,1)}, bf16[512,2048]{1,0:T(8,128)(2,1)}, u32[]{:S(2)}, u32[]{:S(2)}) collective-permute-start(bf16[512,2048]{1,0:T(8,128)(2,1)} %pad_maximum_fusion.2.refs_4_.refs_5_), channel_id=1, source_target_pairs={{1,0},{0,1},{3,2},{2,3},{5,4},{4,5},{7,6},{6,7},{9,8},{8,9},{11,10... | collective-permute-start | bytes 6291464 | tf_op jit(solution)/shard_map/ppermute | solution.py:38
  193.9 26.8 %collective-permute-start.30 = (bf16[512,2048]{1,0:T(8,128)(2,1)}, bf16[512,2048]{1,0:T(8,128)(2,1)}, u32[]{:S(2)}, u32[]{:S(2)}) collective-permute-start(bf16[512,2048]{1,0:T(8,128)(2,1)} %constant_dynamic-update-slice_fusion.refs_4_.refs_5_), channel_id=1, source_target_pairs={{1,0},{0,1},{3,2},{2,3},{5,4},{4,5},{7,6},{6,7},{9,8},{8,9},{11,10... | collective-permute-start | bytes 6291464 | tf_op jit(solution)/shard_map/ppermute | solution.py:38
  243.2 30.7 %collective-permute-start.36 = (bf16[4,1152,128]{2,1,0:T(8,128)(2,1)}, bf16[4,1152,128]{2,1,0:T(8,128)(2,1)S(1)}, u32[]{:S(2)}, u32[]{:S(2)}) collective-permute-start(bf16[4,1152,128]{2,1,0:T(8,128)(2,1)} %get-tuple-element.23), channel_id=1, source_target_pairs={{32,0},{48,16},{0,32},{16,48},{96,64},{112,80},{64,96},{80,112},{1... | collective-permute-start | bytes 3538952 | tf_op jit(solution)/shard_map/ppermute | solution.py:42
  245.4 53.2 %collective-permute-start.37 = (bf16[4,1152,128]{2,1,0:T(8,128)(2,1)}, bf16[4,1152,128]{2,1,0:T(8,128)(2,1)S(1)}, u32[]{:S(2)}, u32[]{:S(2)}) collective-permute-start(bf16[4,1152,128]{2,1,0:T(8,128)(2,1)} %get-tuple-element.24), channel_id=1, source_target_pairs={{48,0},{0,16},{16,32},{32,48},{112,64},{64,80},{80,96},{96,112},{1... | collective-permute-start | bytes 3538952 | tf_op jit(solution)/shard_map/ppermute | solution.py:42
  245.4 53.2 %collective-permute-start.38 = (bf16[4,1152,128]{2,1,0:T(8,128)(2,1)}, bf16[4,1152,128]{2,1,0:T(8,128)(2,1)S(1)}, u32[]{:S(2)}, u32[]{:S(2)}) collective-permute-start(bf16[4,1152,128]{2,1,0:T(8,128)(2,1)} %get-tuple-element.25), channel_id=1, source_target_pairs={{16,0},{32,16},{48,32},{0,48},{80,64},{96,80},{112,96},{64,112},{1... | collective-permute-start | bytes 3538952 | tf_op jit(solution)/shard_map/ppermute | solution.py:42
  247.5 65.6 %collective-permute-start.31 = (bf16[512,2048]{1,0:T(8,128)(2,1)}, bf16[512,2048]{1,0:T(8,128)(2,1)S(1)}, u32[]{:S(2)}, u32[]{:S(2)}) collective-permute-start(bf16[512,2048]{1,0:T(8,128)(2,1)} %fusion.19), channel_id=1, source_target_pairs={{1,0},{0,1},{3,2},{2,3},{5,4},{4,5},{7,6},{6,7},{9,8},{8,9},{11,10... | collective-permute-start | bytes 6291464 | tf_op jit(solution)/shard_map/ppermute | solution.py:38
  250.5 66.2 %collective-permute-start.23 = (bf16[512,2048]{1,0:T(8,128)(2,1)S(1)}, bf16[512,2048]{1,0:T(8,128)(2,1)S(1)}, u32[]{:S(2)}, u32[]{:S(2)}) collective-permute-start(bf16[512,2048]{1,0:T(8,128)(2,1)S(1)} %fusion.16), channel_id=1, source_target_pairs={{1,0},{0,1},{3,2},{2,3},{5,4},{4,5},{7,6},{6,7},{9,8},{8,9},{11,10... | collective-permute-start | bytes 6291464 | tf_op jit(solution)/shard_map/ppermute | solution.py:38
  299.3 43.3 %collective-permute-start.39 = (bf16[1152,128]{1,0:T(8,128)(2,1)S(1)}, bf16[1152,128]{1,0:T(8,128)(2,1)S(1)}, u32[]{:S(2)}, u32[]{:S(2)}) collective-permute-start(bf16[1152,128]{1,0:T(8,128)(2,1)S(1)} %get-tuple-element.71), channel_id=1, source_target_pairs={{128,0},{144,16},{160,32},{176,48},{192,64},{208,80},{224,96},{240... | collective-permute-start | bytes 884744 | tf_op jit(solution)/shard_map/ppermute | solution.py:42
  313.1 32.0 %collective-permute-start.40 = (bf16[1152,128]{1,0:T(8,128)(2,1)S(1)}, bf16[1152,128]{1,0:T(8,128)(2,1)S(1)}, u32[]{:S(2)}, u32[]{:S(2)}) collective-permute-start(bf16[1152,128]{1,0:T(8,128)(2,1)S(1)} %get-tuple-element.73), channel_id=1, source_target_pairs={{192,0},{208,16},{224,32},{240,48},{0,64},{16,80},{32,96},{48,112}... | collective-permute-start | bytes 884744 | tf_op jit(solution)/shard_map/ppermute | solution.py:42
  314.4 25.6 %collective-permute-start.33 = (bf16[128,2048]{1,0:T(8,128)(2,1)S(1)}, bf16[128,2048]{1,0:T(8,128)(2,1)S(1)}, u32[]{:S(2)}, u32[]{:S(2)}) collective-permute-start(bf16[128,2048]{1,0:T(8,128)(2,1)S(1)} %get-tuple-element.53), channel_id=1, source_target_pairs={{12,0},{13,1},{14,2},{15,3},{0,4},{1,5},{2,6},{3,7},{4,8},{5,9},{6... | collective-permute-start | bytes 1572872 | tf_op jit(solution)/shard_map/ppermute | solution.py:38
  316.7 24.0 %collective-permute-start.34 = (bf16[128,2048]{1,0:T(8,128)(2,1)S(1)}, bf16[128,2048]{1,0:T(8,128)(2,1)S(1)}, u32[]{:S(2)}, u32[]{:S(2)}) collective-permute-start(bf16[128,2048]{1,0:T(8,128)(2,1)S(1)} %get-tuple-element.52), channel_id=1, source_target_pairs={{4,0},{5,1},{6,2},{7,3},{8,4},{9,5},{10,6},{11,7},{12,8},{13,9},{1... | collective-permute-start | bytes 1572872 | tf_op jit(solution)/shard_map/ppermute | solution.py:38
  330.1 19.6 %collective-permute-start.41 = (bf16[1152,128]{1,0:T(8,128)(2,1)S(1)}, bf16[1152,128]{1,0:T(8,128)(2,1)S(1)}, u32[]{:S(2)}, u32[]{:S(2)}) collective-permute-start(bf16[1152,128]{1,0:T(8,128)(2,1)S(1)} %get-tuple-element.72), channel_id=1, source_target_pairs={{64,0},{80,16},{96,32},{112,48},{128,64},{144,80},{160,96},{176,11... | collective-permute-start | bytes 884744 | tf_op jit(solution)/shard_map/ppermute | solution.py:42
  340.6 26.2 %collective-permute-start.25 = (bf16[128,2048]{1,0:T(8,128)(2,1)}, bf16[128,2048]{1,0:T(8,128)(2,1)}, u32[]{:S(2)}, u32[]{:S(2)}) collective-permute-start(bf16[128,2048]{1,0:T(8,128)(2,1)} %get-tuple-element.50), channel_id=1, source_target_pairs={{12,0},{13,1},{14,2},{15,3},{0,4},{1,5},{2,6},{3,7},{4,8},{5,9},{6... | collective-permute-start | bytes 1572872 | tf_op jit(solution)/shard_map/ppermute | solution.py:38
  342.6 24.3 %collective-permute-start.26 = (bf16[128,2048]{1,0:T(8,128)(2,1)}, bf16[128,2048]{1,0:T(8,128)(2,1)}, u32[]{:S(2)}, u32[]{:S(2)}) collective-permute-start(bf16[128,2048]{1,0:T(8,128)(2,1)} %get-tuple-element.49), channel_id=1, source_target_pairs={{4,0},{5,1},{6,2},{7,3},{8,4},{9,5},{10,6},{11,7},{12,8},{13,9},{1... | collective-permute-start | bytes 1572872 | tf_op jit(solution)/shard_map/ppermute | solution.py:38
  345.1 28.6 %collective-permute-start.35 = (bf16[128,2048]{1,0:T(8,128)(2,1)}, bf16[128,2048]{1,0:T(8,128)(2,1)}, u32[]{:S(2)}, u32[]{:S(2)}) collective-permute-start(bf16[128,2048]{1,0:T(8,128)(2,1)} %add_convert_fusion.1), channel_id=1, source_target_pairs={{2,0},{3,1},{0,2},{1,3},{6,4},{7,5},{4,6},{5,7},{10,8},{11,9},{8,1... | collective-permute-start | bytes 1572872 | tf_op jit(solution)/shard_map/ppermute | solution.py:38
  (39 other events, 424.6 us)
where the time goes:
time: 385 us; the launch traced here: 377 us
  waiting for transfers between devices  183 us (48%)
  starting transfers between devices  94.6 us (25%)
  matrix products  40.4 us (10%)
  Pallas kernels  28.6 us (7%)
  other arithmetic  19.5 us (5%)
  local copies, waits for them, and re-layouts  9.1 us (2%)
    ppermute x36, waiting for transfers between devices, from_expert(): return lax.ppermute(value, 'expert', expert_perm(dy, dz, dc))  139 us
    ppermute x36, starting transfers between devices, from_expert(): return lax.ppermute(value, 'expert', expert_perm(dy, dz, dc))  69.1 us
    ppermute x6, waiting for transfers between devices, from_dp(): return lax.ppermute(value, 'dp', dp_perm(dzl, dx))  43.9 us
    dot_general x16, matrix products, mm(): return lax.dot_general(a, b, (dims, ((), ())), preferred_element_type=F32)  40.4 us
    pallas_call x2, Pallas kernels, weight_grads(): pl.pallas_call(functools.partial(grad_kernel, first=acc is None), grid_sp...  28.6 us
    ppermute x6, starting transfers between devices, from_dp(): return lax.ppermute(value, 'dp', dp_perm(dzl, dx))  21.8 us
  transfers between devices with their start and end apart: 43, of which 25 were waited for; matrix products, arithmetic and copies ran while one was open for 12% of the time, Pallas kernels for 4%

commit v1 on v0

--- a/solution.py
+++ b/solution.py
@@ -1,5 +1,3 @@
-import functools
-
 import jax
 import jax.numpy as jnp
 from jax import lax
@@ -67,6 +65,7 @@
 
 
 def joined(part, other, rows):
+    (part,) = tie(part.astype(BF))
     got = across(other.astype(BF))
     out = []
     for dy in range(NY):
@@ -78,48 +77,38 @@
 LANES = 128
 
 
-def grad_kernel(x_ref, *refs, first):
-    columns, refs = refs[:8], refs[8:]
-    sides, refs = refs[:6], refs[6:]
-    acc, refs = (None, refs) if first else (refs[0], refs[1:])
-    outs, turned = refs[:-1], refs[-1]
+def grad_kernel(x_ref, *refs):
+    columns, refs = refs[:16], refs[16:]
+    sides, outs, turned = refs[:12], refs[12:-1], refs[-1]
     ff = sides[0].shape[1]
 
     @pl.when((pl.program_id(0) == 0) & (pl.program_id(1) == 0))
     def _():
-        for k in range(6):
+        for k in range(12):
             turned[k] = sides[k][...].astype(F32).T.astype(BF)
 
-    def product(k, at):
-        wide = jnp.concatenate([columns[at][...], columns[at + 1][...]], axis=1)
-        return mm(turned[k], wide, ((1,), (0,)))
-
-    parts = [
-        product(0, 0) + product(3, 2),
-        product(1, 0) + product(4, 2),
-        product(2, 4) + product(5, 6),
+    wide = [
+        jnp.concatenate([columns[2 * k][...], columns[2 * k + 1][...]], axis=1) for k in range(8)
     ]
 
-    def store(out, *lead):
-        for k in range(3):
-            rows = slice(k * ff, (k + 1) * ff)
-            for z in range(2):
-                value = parts[k][:, z * LANES : (z + 1) * LANES]
-                if acc is not None:
-                    value = value + acc[0, z, rows, :]
-                out[(*lead, z, rows, slice(None))] = value.astype(out.dtype)
-
-    if first:
-        store(outs[0], 0)
-    else:
-        for k in range(NX):
-
-            @pl.when(pl.program_id(0) == k)
-            def _(k=k):
-                store(outs[k])
-
-
-def weight_grads(row_blocks, res, sides, acc):
+    def product(side, array):
+        total = mm(turned[side], wide[array], ((1,), (0,)))
+        for p in range(1, 4):
+            total = total + mm(turned[3 * p + side], wide[array + p], ((1,), (0,)))
+        return total.astype(BF)
+
+    parts = [product(0, 0), product(1, 0), product(2, 4)]
+    for k in range(NX):
+
+        @pl.when(pl.program_id(0) == k)
+        def _(k=k):
+            for side in range(3):
+                for z in range(2):
+                    value = parts[side][:, z * LANES : (z + 1) * LANES]
+                    outs[k][z, side * ff : (side + 1) * ff, :] = value
+
+
+def weight_grads(row_blocks, res, sides):
     count, features = row_blocks[0].shape
     ff = sides[0].shape[1]
     x_at = (lax.axis_index("dp") % NX).astype(jnp.int32).reshape(1)
@@ -130,50 +119,49 @@
             lambda i, j, x: (0, (2 * j + second) * NX + (x[0] + i) % NX),
         )
 
+    def block_of(k):
+        def index(i, j, x):
+            return (jnp.where(i == k, j, jnp.where(i < k, 0, 1)), 0, 0)
+
+        return pl.BlockSpec((2, 3 * ff, LANES), index)
+
     args, specs = [], []
     for array in (*row_blocks, *res):
         args += [array, array]
         specs += [column(0), column(1)]
     args += sides
-    specs += [pl.BlockSpec((count, ff), lambda i, j, x: (0, 0))] * 6
-    whole = (NX, NZ, 3 * ff, LANES)
-    acc_spec = pl.BlockSpec((1, 2, 3 * ff, LANES), lambda i, j, x: (i, j, 0, 0))
-    if acc is None:
-        out_specs = [acc_spec]
-        out_shape = [jax.ShapeDtypeStruct(whole, F32)]
-    else:
-        args.append(acc)
-        specs.append(acc_spec)
-
-        def block_of(k):
-            def index(i, j, x):
-                return (jnp.where(i == k, j, jnp.where(i < k, 0, 1)), 0, 0)
-
-            return pl.BlockSpec((2, 3 * ff, LANES), index)
-
-        out_specs = [block_of(k) for k in range(NX)]
-        out_shape = [jax.ShapeDtypeStruct(whole[1:], BF)] * NX
+    specs += [pl.BlockSpec((count, ff), lambda i, j, x: (0, 0))] * 12
     return pl.pallas_call(
-        functools.partial(grad_kernel, first=acc is None),
+        grad_kernel,
         grid_spec=pltpu.PrefetchScalarGridSpec(
             num_scalar_prefetch=1,
             grid=(NX, NZ // 2),
             in_specs=specs,
-            out_specs=out_specs,
-            scratch_shapes=[pltpu.VMEM((6, ff, count), BF)],
+            out_specs=[block_of(k) for k in range(NX)],
+            scratch_shapes=[pltpu.VMEM((12, ff, count), BF)],
         ),
-        out_shape=out_shape,
+        out_shape=[jax.ShapeDtypeStruct((NZ, 3 * ff, LANES), BF)] * NX,
         name="weight_grads",
         cost_estimate=pl.CostEstimate(
-            flops=12 * count * features * ff,
+            flops=24 * count * features * ff,
             transcendentals=0,
-            bytes_accessed=8 * count * features + 24 * features * ff,
+            bytes_accessed=16 * count * features + 12 * features * ff,
         ),
     )(x_at, *args)
 
 
 def x_stage(blocks):
-    return [from_dp(blocks[dx], 0, -dx) for dx in (2, 1, 3)]
+    half = NZ // 2
+    low, high = slice(0, half), slice(half, None)
+    via_low = from_dp(blocks[2][low], 0, -1)
+    via_high = from_dp(blocks[2][high], 0, 1)
+    up_high = from_dp(blocks[1][high], 0, -1)
+    down_low = from_dp(blocks[3][low], 0, 1)
+    up = (blocks[1][low].astype(F32) + via_low.astype(F32)).astype(BF)
+    down = (blocks[3][high].astype(F32) + via_high.astype(F32)).astype(BF)
+    up_low = from_dp(up, 0, -1)
+    down_high = from_dp(down, 0, 1)
+    return [jnp.concatenate([up_low, up_high]), jnp.concatenate([down_low, down_high])]
 
 
 def z_stage(total):
@@ -268,11 +256,11 @@
             out += [back[dc][0], back[dc][1], hidden[dz][dc]]
         return out
 
-    (term,) = weight_grads(row_blocks[0], res, sides(0, near_back), None)
-
-    res = [far_res, across(far_res)]
-    back = [backward(res[dc], saved[1][dc]) for dc in (0, 1)]
-    blocks = weight_grads(row_blocks[1], res, sides(1, back), term)
+    all_res = [*res, far_res, across(far_res)]
+    back = [backward(all_res[2 + dc], saved[1][dc]) for dc in (0, 1)]
+    blocks = weight_grads(
+        [*row_blocks[0], *row_blocks[1]], all_res, sides(0, near_back) + sides(1, back)
+    )
     got = x_stage(blocks)
     far_both = joined(back[0][2], back[1][2], rows)
     far_sum = scatter_y(far_both, far_both[0]).astype(BF)

time: 385 us -> 357 us (0.927)
  the two profiles are of different devices: /device:TPU:2 before, /device:TPU:35 now
where the time goes in v1:
time: 357 us; the launch traced here: 350 us
  waiting for transfers between devices  198 us (55%)
  starting transfers between devices  61.9 us (17%)
  matrix products  38.2 us (11%)
  Pallas kernels  20.7 us (6%)
  other arithmetic  20.1 us (6%)
  local copies, waits for them, and re-layouts  9.58 us (3%)
    ppermute x36, waiting for transfers between devices, from_expert(): return lax.ppermute(value, 'expert', expert_perm(dy, dz, dc))  159 us
    ppermute x36, starting transfers between devices, from_expert(): return lax.ppermute(value, 'expert', expert_perm(dy, dz, dc))  47.8 us
    dot_general x16, matrix products, mm(): return lax.dot_general(a, b, (dims, ((), ())), preferred_element_type=F32)  38.2 us
    ppermute x9, waiting for transfers between devices, from_dp(): return lax.ppermute(value, 'dp', dp_perm(dzl, dx))  36.5 us
    pallas_call x1, Pallas kernels, weight_grads(): pl.pallas_call(grad_kernel, grid_spec=pltpu.PrefetchScalarGridSpec(num_sc...  20.7 us
    ppermute x9, starting transfers between devices, from_dp(): return lax.ppermute(value, 'dp', dp_perm(dzl, dx))  8.81 us
  transfers between devices with their start and end apart: 46, of which 29 were waited for; matrix products, arithmetic and copies ran while one was open for 13% of the time, Pallas kernels for 0%

profile of v1, /device:TPU:35, one launch (start us, length us, event | category | flops | bytes accessed | tf_op | source)
XLA Modules:
  0.0 349.9 jit_solution(10953991814487136080)
XLA Ops:
  4.5 6.0 %collective-permute-start.3 = (bf16[128,2048]{1,0:T(8,128)(2,1)}, bf16[128,2048]{1,0:T(8,128)(2,1)}, u32[]{:S(2)}, u32[]{:S(2)}) collective-permute-start(bf16[128,2048]{1,0:T(8,128)(2,1)} %param.7), channel_id=1, source_target_pairs={{2,0},{3,1},{0,2},{1,3},{6,4},{7,5},{4,6},{5,7},{10,8},{11,9},{8,1... | collective-permute-start | bytes 1572872 | tf_op jit(solution)/shard_map/ppermute | solution.py:36
  12.6 5.3 %all-to-all-start = ((f32[16,1,128]{2,1,0:T(1,128)}), f32[16,1,128]{2,1,0:T(1,128)S(1)}, u32[]{:S(2)}, u32[]{:S(2)}) async-start(f32[16,1,128]{2,1,0:T(1,128)} %bitcast.1), calls=%async_computation | async-start | bytes 16384 | tf_op jit(solution)/shard_map/all_to_all | solution.py:195
  18.0 12.4 %collective-permute-done.2 = bf16[128,2048]{1,0:T(8,128)(2,1)} collective-permute-done((bf16[128,2048]{1,0:T(8,128)(2,1)}, bf16[128,2048]{1,0:T(8,128)(2,1)}, u32[]{:S(2)}, u32[]{:S(2)}) %collective-permute-start.2) | collective-permute-done | bytes 524320 | tf_op jit(solution)/shard_map/ppermute | solution.py:36
  53.7 7.6 %collective-permute-done.4 = bf16[128,2048]{1,0:T(8,128)(2,1)S(1)} collective-permute-done((bf16[128,2048]{1,0:T(8,128)(2,1)}, bf16[128,2048]{1,0:T(8,128)(2,1)S(1)}, u32[]{:S(2)}, u32[]{:S(2)}) %collective-permute-start.4) | collective-permute-done | bytes 524320 | tf_op jit(solution)/shard_map/ppermute | solution.py:36
  64.4 12.0 %collective-permute-done.6 = bf16[128,2048]{1,0:T(8,128)(2,1)S(1)} collective-permute-done((bf16[128,2048]{1,0:T(8,128)(2,1)}, bf16[128,2048]{1,0:T(8,128)(2,1)S(1)}, u32[]{:S(2)}, u32[]{:S(2)}) %collective-permute-start.6) | collective-permute-done | bytes 524320 | tf_op jit(solution)/shard_map/ppermute | solution.py:36
  79.1 3.8 %collective-permute-done.12.refs_6_.refs_7_ = bf16[512,2048]{1,0:T(8,128)(2,1)S(1)} collective-permute-done((bf16[512,2048]{1,0:T(8,128)(2,1)S(1)}, bf16[512,2048]{1,0:T(8,128)(2,1)S(1)}, u32[]{:S(2)}, u32[]{:S(2)}) %collective-permute-start.12) | collective-permute-done | bytes 2097184 | tf_op jit(solution)/shard_map/ppermute | solution.py:36
  97.3 8.6 %collective-permute-done.14 = bf16[128,2048]{1,0:T(8,128)(2,1)S(1)} collective-permute-done((bf16[128,2048]{1,0:T(8,128)(2,1)S(1)}, bf16[128,2048]{1,0:T(8,128)(2,1)S(1)}, u32[]{:S(2)}, u32[]{:S(2)}) %collective-permute-start.14) | collective-permute-done | bytes 524320 | tf_op jit(solution)/shard_map/ppermute | solution.py:36
  106.2 11.6 %collective-permute-done.15 = bf16[128,2048]{1,0:T(8,128)(2,1)S(1)} collective-permute-done((bf16[128,2048]{1,0:T(8,128)(2,1)S(1)}, bf16[128,2048]{1,0:T(8,128)(2,1)S(1)}, u32[]{:S(2)}, u32[]{:S(2)}) %collective-permute-start.15) | collective-permute-done | bytes 524320 | tf_op jit(solution)/shard_map/ppermute | solution.py:36
  118.3 5.3 %collective-permute-start.17 = (bf16[128,2048]{1,0:T(8,128)(2,1)S(1)}, bf16[128,2048]{1,0:T(8,128)(2,1)S(1)}, u32[]{:S(2)}, u32[]{:S(2)}) collective-permute-start(bf16[128,2048]{1,0:T(8,128)(2,1)S(1)} %add_convert_fusion.12), channel_id=1, source_target_pairs={{2,0},{3,1},{0,2},{1,3},{6,4},{7,5},{4,6},{5,7},{10,8},{11,9},{8,1... | collective-permute-start | bytes 1572872 | tf_op jit(solution)/shard_map/ppermute | solution.py:36
  123.6 6.2 %collective-permute-done.10 = bf16[128,2048]{1,0:T(8,128)(2,1)S(1)} collective-permute-done((bf16[128,2048]{1,0:T(8,128)(2,1)S(1)}, bf16[128,2048]{1,0:T(8,128)(2,1)S(1)}, u32[]{:S(2)}, u32[]{:S(2)}) %collective-permute-start.10) | collective-permute-done | bytes 524320 | tf_op jit(solution)/shard_map/ppermute | solution.py:36
  129.8 9.9 %collective-permute-done.9 = bf16[128,2048]{1,0:T(8,128)(2,1)S(1)} collective-permute-done((bf16[128,2048]{1,0:T(8,128)(2,1)S(1)}, bf16[128,2048]{1,0:T(8,128)(2,1)S(1)}, u32[]{:S(2)}, u32[]{:S(2)}) %collective-permute-start.9) | collective-permute-done | bytes 524320 | tf_op jit(solution)/shard_map/ppermute | solution.py:36
  139.6 6.0 %collective-permute-done.17 = bf16[128,2048]{1,0:T(8,128)(2,1)S(1)} collective-permute-done((bf16[128,2048]{1,0:T(8,128)(2,1)S(1)}, bf16[128,2048]{1,0:T(8,128)(2,1)S(1)}, u32[]{:S(2)}, u32[]{:S(2)}) %collective-permute-start.17) | collective-permute-done | bytes 524320 | tf_op jit(solution)/shard_map/ppermute | solution.py:36
  148.4 4.2 %collective-permute-start.21 = (bf16[128,2048]{1,0:T(8,128)(2,1)S(1)}, bf16[128,2048]{1,0:T(8,128)(2,1)S(1)}, u32[]{:S(2)}, u32[]{:S(2)}) collective-permute-start(bf16[128,2048]{1,0:T(8,128)(2,1)S(1)} %get-tuple-element.61), channel_id=1, source_target_pairs={{2,0},{3,1},{0,2},{1,3},{6,4},{7,5},{4,6},{5,7},{10,8},{11,9},{8,1... | collective-permute-start | bytes 1572872 | tf_op jit(solution)/shard_map/ppermute | solution.py:36
  152.6 7.3 %collective-permute-done.18 = bf16[128,2048]{1,0:T(8,128)(2,1)S(1)} collective-permute-done((bf16[128,2048]{1,0:T(8,128)(2,1)S(1)}, bf16[128,2048]{1,0:T(8,128)(2,1)S(1)}, u32[]{:S(2)}, u32[]{:S(2)}) %collective-permute-start.18) | collective-permute-done | bytes 524320 | tf_op jit(solution)/shard_map/ppermute | solution.py:36
  161.8 12.3 %collective-permute-done.20 = bf16[128,2048]{1,0:T(8,128)(2,1)S(1)} collective-permute-done((bf16[128,2048]{1,0:T(8,128)(2,1)S(1)}, bf16[128,2048]{1,0:T(8,128)(2,1)S(1)}, u32[]{:S(2)}, u32[]{:S(2)}) %collective-permute-start.20) | collective-permute-done | bytes 524320 | tf_op jit(solution)/shard_map/ppermute | solution.py:36
  179.1 9.6 %collective-permute-done.27 = bf16[128,2048]{1,0:T(8,128)(2,1)S(1)} collective-permute-done((bf16[128,2048]{1,0:T(8,128)(2,1)S(1)}, bf16[128,2048]{1,0:T(8,128)(2,1)S(1)}, u32[]{:S(2)}, u32[]{:S(2)}) %collective-permute-start.27) | collective-permute-done | bytes 524320 | tf_op jit(solution)/shard_map/ppermute | solution.py:36
  190.5 11.8 %collective-permute-done.29 = bf16[128,2048]{1,0:T(8,128)(2,1)S(1)} collective-permute-done((bf16[128,2048]{1,0:T(8,128)(2,1)S(1)}, bf16[128,2048]{1,0:T(8,128)(2,1)S(1)}, u32[]{:S(2)}, u32[]{:S(2)}) %collective-permute-start.29) | collective-permute-done | bytes 524320 | tf_op jit(solution)/shard_map/ppermute | solution.py:36
  203.8 5.0 %multiply_convert_fusion.7 = (bf16[512,384]{1,0:T(8,128)(2,1)}, bf16[512,384]{1,0:T(8,128)(2,1)}) fusion(f32[512,768]{1,0:T(8,128)} %copy-done.13, bf16[512,2048]{1,0:T(8,128)(2,1)} %pad_maximum_fusion.2.refs_8_.refs_9_, bf16[1,384,2048]{2,1,0:T(8,128)(2,1)} %param.13, f32[512]{0:T(512)S(1)} %get-tuple-element.76), kind=kOutput, calls=%fused_computation.86 | convolution fusion | flops 808058880 | bytes 6031360 | tf_op jit(solution)/shard_map/dot_general | solution.py:44
  208.8 4.1 %multiply_convert_fusion.3 = (bf16[512,384]{1,0:T(8,128)(2,1)}, bf16[512,384]{1,0:T(8,128)(2,1)}) fusion(f32[512,768]{1,0:T(8,128)S(1)} %copy-done.17, bf16[512,2048]{1,0:T(8,128)(2,1)} %constant_dynamic-update-slice_fusion.refs_12_.refs_13_, bf16[1,384,2048]{2,1,0:T(8,128)(2,1)S(1)} %copy-done.31, f32[512]{0:T(512)S(1)} %get-tuple-element.78), kind=kOutput, calls=%fused_computation.82 | convolution fusion | flops 808058880 | bytes 6031360 | tf_op jit(solution)/shard_map/dot_general | solution.py:44
  212.9 4.1 %multiply_convert_fusion.5 = (bf16[512,384]{1,0:T(8,128)(2,1)}, bf16[512,384]{1,0:T(8,128)(2,1)}) fusion(f32[512,768]{1,0:T(8,128)S(1)} %copy-done.12, bf16[512,2048]{1,0:T(8,128)(2,1)} %collective-permute-done.22.refs_10_.refs_11_, bf16[1,384,2048]{2,1,0:T(8,128)(2,1)S(1)} %copy-done.31, f32[512]{0:T(512)S(1)} %get-tuple-element.77), kind=kOutput, calls=%fused_computation.84 | convolution fusion | flops 808058880 | bytes 6031360 | tf_op jit(solution)/shard_map/dot_general | solution.py:44
  217.0 3.9 %multiply_convert_fusion.1 = (bf16[512,384]{1,0:T(8,128)(2,1)}, bf16[512,384]{1,0:T(8,128)(2,1)}) fusion(f32[512,768]{1,0:T(8,128)S(1)} %copy-done.15, bf16[512,2048]{1,0:T(8,128)(2,1)} %collective-permute-done.30.refs_14_.refs_15_, bf16[1,384,2048]{2,1,0:T(8,128)(2,1)S(1)} %copy-done.31, f32[512]{0:T(512)S(1)} %get-tuple-element.79), kind=kOutput, calls=%fused_computation.80 | convolution fusion | flops 808058880 | bytes 6031360 | tf_op jit(solution)/shard_map/dot_general | solution.py:44
  221.0 20.7 %weight_grads.1 = (bf16[4,1152,128]{2,1,0:T(8,128)(2,1)}, bf16[4,1152,128]{2,1,0:T(8,128)(2,1)}, bf16[4,1152,128]{2,1,0:T(8,128)(2,1)}, bf16[4,1152,128]{2,1,0:T(8,128)(2,1)}) custom-call(s32[1]{0:T(128)} %bitcast.5.x_ref, bf16[512,2048]{1,0:T(8,128)(2,1)} %pad_maximum_fusion.refs_0_.refs_1_, bf16[512,2048]{1,0:T(8,128)(2,1)} %pad_maximum_fusion.refs_0_.refs_1_, ...), custom_call_target="tpu_custom_call" | custom-call | flops 9663676416 | bytes 26214400 | tf_op jit(solution)/shard_map/weight_grads/pallas_call | solution.py:134
  250.8 7.2 %collective-permute-done.36 = bf16[2,1152,128]{2,1,0:T(8,128)(2,1)S(1)} collective-permute-done((bf16[2,1152,128]{2,1,0:T(8,128)(2,1)S(1)}, bf16[2,1152,128]{2,1,0:T(8,128)(2,1)S(1)}, u32[]{:S(2)}, u32[]{:S(2)}) %collective-permute-start.36) | collective-permute-done | bytes 589856 | tf_op jit(solution)/shard_map/ppermute | solution.py:40
  262.8 7.8 %collective-permute-done.38 = bf16[2,1152,128]{2,1,0:T(8,128)(2,1)S(1)} collective-permute-done((bf16[2,1152,128]{2,1,0:T(8,128)(2,1)S(1)}, bf16[2,1152,128]{2,1,0:T(8,128)(2,1)S(1)}, u32[]{:S(2)}, u32[]{:S(2)}) %collective-permute-start.38) | collective-permute-done | bytes 589856 | tf_op jit(solution)/shard_map/ppermute | solution.py:40
  275.7 7.5 %collective-permute-done.37 = bf16[2,1152,128]{2,1,0:T(8,128)(2,1)S(1)} collective-permute-done((bf16[2,1152,128]{2,1,0:T(8,128)(2,1)S(1)}, bf16[2,1152,128]{2,1,0:T(8,128)(2,1)S(1)}, u32[]{:S(2)}, u32[]{:S(2)}) %collective-permute-start.37) | collective-permute-done | bytes 589856 | tf_op jit(solution)/shard_map/ppermute | solution.py:40
  283.2 3.7 %collective-permute-done.41 = bf16[2,1152,128]{2,1,0:T(8,128)(2,1)S(1)} collective-permute-done((bf16[2,1152,128]{2,1,0:T(8,128)(2,1)S(1)}, bf16[2,1152,128]{2,1,0:T(8,128)(2,1)S(1)}, u32[]{:S(2)}, u32[]{:S(2)}) %collective-permute-start.41) | collective-permute-done | bytes 589856 | tf_op jit(solution)/shard_map/ppermute | solution.py:40
  295.5 6.7 %collective-permute-done.32 = bf16[128,2048]{1,0:T(8,128)(2,1)S(1)} collective-permute-done((bf16[128,2048]{1,0:T(8,128)(2,1)S(1)}, bf16[128,2048]{1,0:T(8,128)(2,1)S(1)}, u32[]{:S(2)}, u32[]{:S(2)}) %collective-permute-start.32) | collective-permute-done | bytes 524320 | tf_op jit(solution)/shard_map/ppermute | solution.py:36
  302.2 12.1 %collective-permute-done.33 = bf16[128,2048]{1,0:T(8,128)(2,1)S(1)} collective-permute-done((bf16[128,2048]{1,0:T(8,128)(2,1)S(1)}, bf16[128,2048]{1,0:T(8,128)(2,1)S(1)}, u32[]{:S(2)}, u32[]{:S(2)}) %collective-permute-start.33) | collective-permute-done | bytes 524320 | tf_op jit(solution)/shard_map/ppermute | solution.py:36
  318.7 4.2 %collective-permute-start.35 = (bf16[128,2048]{1,0:T(8,128)(2,1)}, bf16[128,2048]{1,0:T(8,128)(2,1)}, u32[]{:S(2)}, u32[]{:S(2)}) collective-permute-start(bf16[128,2048]{1,0:T(8,128)(2,1)} %add_convert_fusion.3), channel_id=1, source_target_pairs={{2,0},{3,1},{0,2},{1,3},{6,4},{7,5},{4,6},{5,7},{10,8},{11,9},{8,1... | collective-permute-start | bytes 1572872 | tf_op jit(solution)/shard_map/ppermute | solution.py:36
  322.9 8.3 %collective-permute-done.44 = bf16[1152,128]{1,0:T(8,128)(2,1)S(1)} collective-permute-done((bf16[1152,128]{1,0:T(8,128)(2,1)S(1)}, bf16[1152,128]{1,0:T(8,128)(2,1)S(1)}, u32[]{:S(2)}, u32[]{:S(2)}) %collective-permute-start.44) | collective-permute-done | bytes 294944 | tf_op jit(solution)/shard_map/ppermute | solution.py:40
  334.7 6.5 %collective-permute-done.25 = bf16[128,2048]{1,0:T(8,128)(2,1)} collective-permute-done((bf16[128,2048]{1,0:T(8,128)(2,1)}, bf16[128,2048]{1,0:T(8,128)(2,1)}, u32[]{:S(2)}, u32[]{:S(2)}) %collective-permute-start.25) | collective-permute-done | bytes 524320 | tf_op jit(solution)/shard_map/ppermute | solution.py:36
  341.2 5.1 %collective-permute-done.35 = bf16[128,2048]{1,0:T(8,128)(2,1)} collective-permute-done((bf16[128,2048]{1,0:T(8,128)(2,1)}, bf16[128,2048]{1,0:T(8,128)(2,1)}, u32[]{:S(2)}, u32[]{:S(2)}) %collective-permute-start.35) | collective-permute-done | bytes 524320 | tf_op jit(solution)/shard_map/ppermute | solution.py:36
  (192 shorter events, 101.4 us)
Async XLA Ops:
  0.6 17.3 %collective-permute-start = (bf16[128,2048]{1,0:T(8,128)(2,1)}, bf16[128,2048]{1,0:T(8,128)(2,1)}, u32[]{:S(2)}, u32[]{:S(2)}) collective-permute-start(bf16[128,2048]{1,0:T(8,128)(2,1)} %param.7), channel_id=1, source_target_pairs={{4,0},{5,1},{6,2},{7,3},{8,4},{9,5},{10,6},{11,7},{12,8},{13,9},{1... | collective-permute-start | bytes 1572872 | tf_op jit(solution)/shard_map/ppermute | solution.py:36
  3.8 26.6 %collective-permute-start.2 = (bf16[128,2048]{1,0:T(8,128)(2,1)}, bf16[128,2048]{1,0:T(8,128)(2,1)}, u32[]{:S(2)}, u32[]{:S(2)}) collective-permute-start(bf16[128,2048]{1,0:T(8,128)(2,1)} %param.7), channel_id=1, source_target_pairs={{12,0},{13,1},{14,2},{15,3},{0,4},{1,5},{2,6},{3,7},{4,8},{5,9},{6... | collective-permute-start | bytes 1572872 | tf_op jit(solution)/shard_map/ppermute | solution.py:36
  4.5 31.7 %collective-permute-start.3 = (bf16[128,2048]{1,0:T(8,128)(2,1)}, bf16[128,2048]{1,0:T(8,128)(2,1)}, u32[]{:S(2)}, u32[]{:S(2)}) collective-permute-start(bf16[128,2048]{1,0:T(8,128)(2,1)} %param.7), channel_id=1, source_target_pairs={{2,0},{3,1},{0,2},{1,3},{6,4},{7,5},{4,6},{5,7},{10,8},{11,9},{8,1... | collective-permute-start | bytes 1572872 | tf_op jit(solution)/shard_map/ppermute | solution.py:36
  12.6 23.6 %all-to-all-start = ((f32[16,1,128]{2,1,0:T(1,128)}), f32[16,1,128]{2,1,0:T(1,128)S(1)}, u32[]{:S(2)}, u32[]{:S(2)}) async-start(f32[16,1,128]{2,1,0:T(1,128)} %bitcast.1), calls=%async_computation | async-start | bytes 16384 | tf_op jit(solution)/shard_map/all_to_all | solution.py:195
  47.1 30.5 %collective-permute-start.8 = (bf16[512,2048]{1,0:T(8,128)(2,1)S(1)}, bf16[512,2048]{1,0:T(8,128)(2,1)S(1)}, u32[]{:S(2)}, u32[]{:S(2)}) collective-permute-start(bf16[512,2048]{1,0:T(8,128)(2,1)S(1)} %convolution_convert_fusion.2), channel_id=1, source_target_pairs={{1,0},{0,1},{3,2},{2,3},{5,4},{4,5},{7,6},{6,7},{9,8},{8,9},{11,10... | collective-permute-start | bytes 6291464 | tf_op jit(solution)/shard_map/ppermute | solution.py:36
  49.9 26.4 %collective-permute-start.6 = (bf16[128,2048]{1,0:T(8,128)(2,1)}, bf16[128,2048]{1,0:T(8,128)(2,1)S(1)}, u32[]{:S(2)}, u32[]{:S(2)}) collective-permute-start(bf16[128,2048]{1,0:T(8,128)(2,1)} %collective-permute-done.3), channel_id=1, source_target_pairs={{12,0},{13,1},{14,2},{15,3},{0,4},{1,5},{2,6},{3,7},{4,8},{5,9},{6... | collective-permute-start | bytes 1572872 | tf_op jit(solution)/shard_map/ppermute | solution.py:36
  91.6 26.2 %collective-permute-start.15 = (bf16[128,2048]{1,0:T(8,128)(2,1)S(1)}, bf16[128,2048]{1,0:T(8,128)(2,1)S(1)}, u32[]{:S(2)}, u32[]{:S(2)}) collective-permute-start(bf16[128,2048]{1,0:T(8,128)(2,1)S(1)} %get-tuple-element.60), channel_id=1, source_target_pairs={{12,0},{13,1},{14,2},{15,3},{0,4},{1,5},{2,6},{3,7},{4,8},{5,9},{6... | collective-permute-start | bytes 1572872 | tf_op jit(solution)/shard_map/ppermute | solution.py:36
  92.1 25.7 %collective-permute-start.16 = (bf16[128,2048]{1,0:T(8,128)(2,1)S(1)}, bf16[128,2048]{1,0:T(8,128)(2,1)S(1)}, u32[]{:S(2)}, u32[]{:S(2)}) collective-permute-start(bf16[128,2048]{1,0:T(8,128)(2,1)S(1)} %get-tuple-element.59), channel_id=1, source_target_pairs={{4,0},{5,1},{6,2},{7,3},{8,4},{9,5},{10,6},{11,7},{12,8},{13,9},{1... | collective-permute-start | bytes 1572872 | tf_op jit(solution)/shard_map/ppermute | solution.py:36
  94.7 35.1 %collective-permute-start.10 = (bf16[128,2048]{1,0:T(8,128)(2,1)S(1)}, bf16[128,2048]{1,0:T(8,128)(2,1)S(1)}, u32[]{:S(2)}, u32[]{:S(2)}) collective-permute-start(bf16[128,2048]{1,0:T(8,128)(2,1)S(1)} %get-tuple-element.56), channel_id=1, source_target_pairs={{12,0},{13,1},{14,2},{15,3},{0,4},{1,5},{2,6},{3,7},{4,8},{5,9},{6... | collective-permute-start | bytes 1572872 | tf_op jit(solution)/shard_map/ppermute | solution.py:36
  94.7 35.1 %collective-permute-start.11 = (bf16[128,2048]{1,0:T(8,128)(2,1)S(1)}, bf16[128,2048]{1,0:T(8,128)(2,1)S(1)}, u32[]{:S(2)}, u32[]{:S(2)}) collective-permute-start(bf16[128,2048]{1,0:T(8,128)(2,1)S(1)} %get-tuple-element.55), channel_id=1, source_target_pairs={{4,0},{5,1},{6,2},{7,3},{8,4},{9,5},{10,6},{11,7},{12,8},{13,9},{1... | collective-permute-start | bytes 1572872 | tf_op jit(solution)/shard_map/ppermute | solution.py:36
  105.9 33.7 %collective-permute-start.9 = (bf16[128,2048]{1,0:T(8,128)(2,1)S(1)}, bf16[128,2048]{1,0:T(8,128)(2,1)S(1)}, u32[]{:S(2)}, u32[]{:S(2)}) collective-permute-start(bf16[128,2048]{1,0:T(8,128)(2,1)S(1)} %get-tuple-element.54), channel_id=1, source_target_pairs={{8,0},{9,1},{10,2},{11,3},{12,4},{13,5},{14,6},{15,7},{0,8},{1,9},... | collective-permute-start | bytes 1572872 | tf_op jit(solution)/shard_map/ppermute | solution.py:36
  118.3 27.4 %collective-permute-start.17 = (bf16[128,2048]{1,0:T(8,128)(2,1)S(1)}, bf16[128,2048]{1,0:T(8,128)(2,1)S(1)}, u32[]{:S(2)}, u32[]{:S(2)}) collective-permute-start(bf16[128,2048]{1,0:T(8,128)(2,1)S(1)} %add_convert_fusion.12), channel_id=1, source_target_pairs={{2,0},{3,1},{0,2},{1,3},{6,4},{7,5},{4,6},{5,7},{10,8},{11,9},{8,1... | collective-permute-start | bytes 1572872 | tf_op jit(solution)/shard_map/ppermute | solution.py:36
  147.6 26.5 %collective-permute-start.20 = (bf16[128,2048]{1,0:T(8,128)(2,1)S(1)}, bf16[128,2048]{1,0:T(8,128)(2,1)S(1)}, u32[]{:S(2)}, u32[]{:S(2)}) collective-permute-start(bf16[128,2048]{1,0:T(8,128)(2,1)S(1)} %get-tuple-element.61), channel_id=1, source_target_pairs={{12,0},{13,1},{14,2},{15,3},{0,4},{1,5},{2,6},{3,7},{4,8},{5,9},{6... | collective-permute-start | bytes 1572872 | tf_op jit(solution)/shard_map/ppermute | solution.py:36
  148.4 27.3 %collective-permute-start.21 = (bf16[128,2048]{1,0:T(8,128)(2,1)S(1)}, bf16[128,2048]{1,0:T(8,128)(2,1)S(1)}, u32[]{:S(2)}, u32[]{:S(2)}) collective-permute-start(bf16[128,2048]{1,0:T(8,128)(2,1)S(1)} %get-tuple-element.61), channel_id=1, source_target_pairs={{2,0},{3,1},{0,2},{1,3},{6,4},{7,5},{4,6},{5,7},{10,8},{11,9},{8,1... | collective-permute-start | bytes 1572872 | tf_op jit(solution)/shard_map/ppermute | solution.py:36
  175.8 26.5 %collective-permute-start.29 = (bf16[128,2048]{1,0:T(8,128)(2,1)S(1)}, bf16[128,2048]{1,0:T(8,128)(2,1)S(1)}, u32[]{:S(2)}, u32[]{:S(2)}) collective-permute-start(bf16[128,2048]{1,0:T(8,128)(2,1)S(1)} %collective-permute-done.21), channel_id=1, source_target_pairs={{12,0},{13,1},{14,2},{15,3},{0,4},{1,5},{2,6},{3,7},{4,8},{5,9},{6... | collective-permute-start | bytes 1572872 | tf_op jit(solution)/shard_map/ppermute | solution.py:36
  178.0 34.9 %collective-permute-start.22 = (bf16[512,2048]{1,0:T(8,128)(2,1)}, bf16[512,2048]{1,0:T(8,128)(2,1)}, u32[]{:S(2)}, u32[]{:S(2)}) collective-permute-start(bf16[512,2048]{1,0:T(8,128)(2,1)} %pad_maximum_fusion.2.refs_8_.refs_9_), channel_id=1, source_target_pairs={{1,0},{0,1},{3,2},{2,3},{5,4},{4,5},{7,6},{6,7},{9,8},{8,9},{11,10... | collective-permute-start | bytes 6291464 | tf_op jit(solution)/shard_map/ppermute | solution.py:36
  246.2 44.8 %collective-permute-start.23 = (bf16[512,2048]{1,0:T(8,128)(2,1)S(1)}, bf16[512,2048]{1,0:T(8,128)(2,1)S(1)}, u32[]{:S(2)}, u32[]{:S(2)}) collective-permute-start(bf16[512,2048]{1,0:T(8,128)(2,1)S(1)} %fusion.19), channel_id=1, source_target_pairs={{1,0},{0,1},{3,2},{2,3},{5,4},{4,5},{7,6},{6,7},{9,8},{8,9},{11,10... | collective-permute-start | bytes 6291464 | tf_op jit(solution)/shard_map/ppermute | solution.py:36
  246.7 14.9 %collective-permute-start.40 = (bf16[2,1152,128]{2,1,0:T(8,128)(2,1)S(1)}, bf16[2,1152,128]{2,1,0:T(8,128)(2,1)S(1)}, u32[]{:S(2)}, u32[]{:S(2)}) collective-permute-start(bf16[2,1152,128]{2,1,0:T(8,128)(2,1)S(1)} %get-tuple-element.75), channel_id=1, source_target_pairs={{16,0},{32,16},{48,32},{0,48},{80,64},{96,80},{112,96},{64,112},{1... | collective-permute-start | bytes 1769480 | tf_op jit(solution)/shard_map/ppermute | solution.py:40
  249.0 21.5 %collective-permute-start.38 = (bf16[2,1152,128]{2,1,0:T(8,128)(2,1)S(1)}, bf16[2,1152,128]{2,1,0:T(8,128)(2,1)S(1)}, u32[]{:S(2)}, u32[]{:S(2)}) collective-permute-start(bf16[2,1152,128]{2,1,0:T(8,128)(2,1)S(1)} %slice.194), channel_id=1, source_target_pairs={{48,0},{0,16},{16,32},{32,48},{112,64},{64,80},{80,96},{96,112},{1... | collective-permute-start | bytes 1769480 | tf_op jit(solution)/shard_map/ppermute | solution.py:40
  250.4 25.4 %collective-permute-start.39 = (bf16[2,1152,128]{2,1,0:T(8,128)(2,1)S(1)}, bf16[2,1152,128]{2,1,0:T(8,128)(2,1)S(1)}, u32[]{:S(2)}, u32[]{:S(2)}) collective-permute-start(bf16[2,1152,128]{2,1,0:T(8,128)(2,1)S(1)} %slice.195), channel_id=1, source_target_pairs={{16,0},{32,16},{48,32},{0,48},{80,64},{96,80},{112,96},{64,112},{1... | collective-permute-start | bytes 1769480 | tf_op jit(solution)/shard_map/ppermute | solution.py:40
  257.9 29.5 %collective-permute-start.31 = (bf16[512,2048]{1,0:T(8,128)(2,1)S(1)}, bf16[512,2048]{1,0:T(8,128)(2,1)S(1)}, u32[]{:S(2)}, u32[]{:S(2)}) collective-permute-start(bf16[512,2048]{1,0:T(8,128)(2,1)S(1)} %fusion.25), channel_id=1, source_target_pairs={{1,0},{0,1},{3,2},{2,3},{5,4},{4,5},{7,6},{6,7},{9,8},{8,9},{11,10... | collective-permute-start | bytes 6291464 | tf_op jit(solution)/shard_map/ppermute | solution.py:36
  261.7 21.5 %collective-permute-start.37 = (bf16[2,1152,128]{2,1,0:T(8,128)(2,1)S(1)}, bf16[2,1152,128]{2,1,0:T(8,128)(2,1)S(1)}, u32[]{:S(2)}, u32[]{:S(2)}) collective-permute-start(bf16[2,1152,128]{2,1,0:T(8,128)(2,1)S(1)} %add_convert_fusion.1), channel_id=1, source_target_pairs={{48,0},{0,16},{16,32},{32,48},{112,64},{64,80},{80,96},{96,112},{1... | collective-permute-start | bytes 1769480 | tf_op jit(solution)/shard_map/ppermute | solution.py:40
  270.6 16.4 %collective-permute-start.41 = (bf16[2,1152,128]{2,1,0:T(8,128)(2,1)S(1)}, bf16[2,1152,128]{2,1,0:T(8,128)(2,1)S(1)}, u32[]{:S(2)}, u32[]{:S(2)}) collective-permute-start(bf16[2,1152,128]{2,1,0:T(8,128)(2,1)S(1)} %add_convert_fusion), channel_id=1, source_target_pairs={{16,0},{32,16},{48,32},{0,48},{80,64},{96,80},{112,96},{64,112},{1... | collective-permute-start | bytes 1769480 | tf_op jit(solution)/shard_map/ppermute | solution.py:40
  288.2 26.1 %collective-permute-start.33 = (bf16[128,2048]{1,0:T(8,128)(2,1)S(1)}, bf16[128,2048]{1,0:T(8,128)(2,1)S(1)}, u32[]{:S(2)}, u32[]{:S(2)}) collective-permute-start(bf16[128,2048]{1,0:T(8,128)(2,1)S(1)} %get-tuple-element.53), channel_id=1, source_target_pairs={{12,0},{13,1},{14,2},{15,3},{0,4},{1,5},{2,6},{3,7},{4,8},{5,9},{6... | collective-permute-start | bytes 1572872 | tf_op jit(solution)/shard_map/ppermute | solution.py:36
  290.4 24.4 %collective-permute-start.34 = (bf16[128,2048]{1,0:T(8,128)(2,1)S(1)}, bf16[128,2048]{1,0:T(8,128)(2,1)S(1)}, u32[]{:S(2)}, u32[]{:S(2)}) collective-permute-start(bf16[128,2048]{1,0:T(8,128)(2,1)S(1)} %get-tuple-element.52), channel_id=1, source_target_pairs={{4,0},{5,1},{6,2},{7,3},{8,4},{9,5},{10,6},{11,7},{12,8},{13,9},{1... | collective-permute-start | bytes 1572872 | tf_op jit(solution)/shard_map/ppermute | solution.py:36
  290.9 25.1 %collective-permute-start.42 = (bf16[1152,128]{1,0:T(8,128)(2,1)S(1)}, bf16[1152,128]{1,0:T(8,128)(2,1)S(1)}, u32[]{:S(2)}, u32[]{:S(2)}) collective-permute-start(bf16[1152,128]{1,0:T(8,128)(2,1)S(1)} %get-tuple-element.71), channel_id=1, source_target_pairs={{128,0},{144,16},{160,32},{176,48},{192,64},{208,80},{224,96},{240... | collective-permute-start | bytes 884744 | tf_op jit(solution)/shard_map/ppermute | solution.py:40
  291.1 27.6 %collective-permute-start.43 = (bf16[1152,128]{1,0:T(8,128)(2,1)S(1)}, bf16[1152,128]{1,0:T(8,128)(2,1)S(1)}, u32[]{:S(2)}, u32[]{:S(2)}) collective-permute-start(bf16[1152,128]{1,0:T(8,128)(2,1)S(1)} %get-tuple-element.73), channel_id=1, source_target_pairs={{192,0},{208,16},{224,32},{240,48},{0,64},{16,80},{32,96},{48,112}... | collective-permute-start | bytes 884744 | tf_op jit(solution)/shard_map/ppermute | solution.py:40
  302.2 29.0 %collective-permute-start.44 = (bf16[1152,128]{1,0:T(8,128)(2,1)S(1)}, bf16[1152,128]{1,0:T(8,128)(2,1)S(1)}, u32[]{:S(2)}, u32[]{:S(2)}) collective-permute-start(bf16[1152,128]{1,0:T(8,128)(2,1)S(1)} %get-tuple-element.72), channel_id=1, source_target_pairs={{64,0},{80,16},{96,32},{112,48},{128,64},{144,80},{160,96},{176,11... | collective-permute-start | bytes 884744 | tf_op jit(solution)/shard_map/ppermute | solution.py:40
  314.3 20.4 %collective-permute-start.24 = (bf16[128,2048]{1,0:T(8,128)(2,1)}, bf16[128,2048]{1,0:T(8,128)(2,1)}, u32[]{:S(2)}, u32[]{:S(2)}) collective-permute-start(bf16[128,2048]{1,0:T(8,128)(2,1)} %get-tuple-element.48), channel_id=1, source_target_pairs={{8,0},{9,1},{10,2},{11,3},{12,4},{13,5},{14,6},{15,7},{0,8},{1,9},... | collective-permute-start | bytes 1572872 | tf_op jit(solution)/shard_map/ppermute | solution.py:36
  314.8 26.4 %collective-permute-start.25 = (bf16[128,2048]{1,0:T(8,128)(2,1)}, bf16[128,2048]{1,0:T(8,128)(2,1)}, u32[]{:S(2)}, u32[]{:S(2)}) collective-permute-start(bf16[128,2048]{1,0:T(8,128)(2,1)} %get-tuple-element.50), channel_id=1, source_target_pairs={{12,0},{13,1},{14,2},{15,3},{0,4},{1,5},{2,6},{3,7},{4,8},{5,9},{6... | collective-permute-start | bytes 1572872 | tf_op jit(solution)/shard_map/ppermute | solution.py:36
  316.0 25.2 %collective-permute-start.26 = (bf16[128,2048]{1,0:T(8,128)(2,1)}, bf16[128,2048]{1,0:T(8,128)(2,1)}, u32[]{:S(2)}, u32[]{:S(2)}) collective-permute-start(bf16[128,2048]{1,0:T(8,128)(2,1)} %get-tuple-element.49), channel_id=1, source_target_pairs={{4,0},{5,1},{6,2},{7,3},{8,4},{9,5},{10,6},{11,7},{12,8},{13,9},{1... | collective-permute-start | bytes 1572872 | tf_op jit(solution)/shard_map/ppermute | solution.py:36
  318.7 27.6 %collective-permute-start.35 = (bf16[128,2048]{1,0:T(8,128)(2,1)}, bf16[128,2048]{1,0:T(8,128)(2,1)}, u32[]{:S(2)}, u32[]{:S(2)}) collective-permute-start(bf16[128,2048]{1,0:T(8,128)(2,1)} %add_convert_fusion.3), channel_id=1, source_target_pairs={{2,0},{3,1},{0,2},{1,3},{6,4},{7,5},{4,6},{5,7},{10,8},{11,9},{8,1... | collective-permute-start | bytes 1572872 | tf_op jit(solution)/shard_map/ppermute | solution.py:36
  (46 other events, 439.9 us)

commit v2 on v1

--- a/solution.py
+++ b/solution.py
@@ -1,3 +1,5 @@
+import functools
+
 import jax
 import jax.numpy as jnp
 from jax import lax
@@ -77,75 +79,62 @@
 LANES = 128
 
 
-def grad_kernel(x_ref, *refs):
-    columns, refs = refs[:16], refs[16:]
-    sides, outs, turned = refs[:12], refs[12:-1], refs[-1]
+def grad_kernel(x_ref, *refs, first):
+    rows, res, sides = refs[:2], refs[2:4], refs[4:10]
+    acc, refs = (None, refs[10:]) if first else (refs[10], refs[11:])
+    out, turned = refs
     ff = sides[0].shape[1]
 
-    @pl.when((pl.program_id(0) == 0) & (pl.program_id(1) == 0))
+    @pl.when(pl.program_id(0) == 0)
     def _():
-        for k in range(12):
+        for k in range(6):
             turned[k] = sides[k][...].astype(F32).T.astype(BF)
 
-    wide = [
-        jnp.concatenate([columns[2 * k][...], columns[2 * k + 1][...]], axis=1) for k in range(8)
-    ]
-
-    def product(side, array):
-        total = mm(turned[side], wide[array], ((1,), (0,)))
-        for p in range(1, 4):
-            total = total + mm(turned[3 * p + side], wide[array + p], ((1,), (0,)))
-        return total.astype(BF)
-
-    parts = [product(0, 0), product(1, 0), product(2, 4)]
-    for k in range(NX):
-
-        @pl.when(pl.program_id(0) == k)
-        def _(k=k):
-            for side in range(3):
-                for z in range(2):
-                    value = parts[side][:, z * LANES : (z + 1) * LANES]
-                    outs[k][z, side * ff : (side + 1) * ff, :] = value
-
-
-def weight_grads(row_blocks, res, sides):
+    for side in range(3):
+        right = res if side == 2 else rows
+        at = slice(side * ff, (side + 1) * ff)
+        total = mm(turned[side], right[0][...], ((1,), (0,)))
+        total = total + mm(turned[3 + side], right[1][...], ((1,), (0,)))
+        if first:
+            out[at, :] = total
+        else:
+            total = (total + acc[at, :]).astype(BF)
+            for x in range(NX):
+                out[lax.rem(x - x_ref[0] + NX, NX), 0, at, :] = total[:, x * LANES : (x + 1) * LANES]
+
+
+def weight_grads(row_blocks, res, sides, acc):
     count, features = row_blocks[0].shape
     ff = sides[0].shape[1]
+    tile = NX * LANES
     x_at = (lax.axis_index("dp") % NX).astype(jnp.int32).reshape(1)
-
-    def column(second):
-        return pl.BlockSpec(
-            (count, LANES),
-            lambda i, j, x: (0, (2 * j + second) * NX + (x[0] + i) % NX),
-        )
-
-    def block_of(k):
-        def index(i, j, x):
-            return (jnp.where(i == k, j, jnp.where(i < k, 0, 1)), 0, 0)
-
-        return pl.BlockSpec((2, 3 * ff, LANES), index)
-
-    args, specs = [], []
-    for array in (*row_blocks, *res):
-        args += [array, array]
-        specs += [column(0), column(1)]
-    args += sides
-    specs += [pl.BlockSpec((count, ff), lambda i, j, x: (0, 0))] * 12
+    args = [*row_blocks, *res, *sides]
+    specs = [pl.BlockSpec((count, tile), lambda j, x: (0, j))] * 4
+    specs += [pl.BlockSpec((count, ff), lambda j, x: (0, 0))] * 6
+    acc_spec = pl.BlockSpec((3 * ff, tile), lambda j, x: (0, j))
+    if acc is None:
+        out_spec = acc_spec
+        out_shape = jax.ShapeDtypeStruct((3 * ff, features), F32)
+    else:
+        args.append(acc)
+        specs.append(acc_spec)
+        out_spec = pl.BlockSpec((NX, 1, 3 * ff, LANES), lambda j, x: (0, j, 0, 0))
+        out_shape = jax.ShapeDtypeStruct((NX, NZ, 3 * ff, LANES), BF)
     return pl.pallas_call(
-        grad_kernel,
+        functools.partial(grad_kernel, first=acc is None),
         grid_spec=pltpu.PrefetchScalarGridSpec(
             num_scalar_prefetch=1,
-            grid=(NX, NZ // 2),
+            grid=(NZ,),
             in_specs=specs,
-            out_specs=[block_of(k) for k in range(NX)],
-            scratch_shapes=[pltpu.VMEM((12, ff, count), BF)],
+            out_specs=out_spec,
+            scratch_shapes=[pltpu.VMEM((6, ff, count), BF)],
         ),
-        out_shape=[jax.ShapeDtypeStruct((NZ, 3 * ff, LANES), BF)] * NX,
+        out_shape=out_shape,
         name="weight_grads",
         cost_estimate=pl.CostEstimate(
-            flops=24 * count * features * ff,
+            flops=12 * count * features * ff,
             transcendentals=0,
-            bytes_accessed=16 * count * features + 12 * features * ff,
+            bytes_accessed=8 * count * features + 18 * features * ff,
         ),
     )(x_at, *args)
 
@@ -256,11 +245,11 @@
             out += [back[dc][0], back[dc][1], hidden[dz][dc]]
         return out
 
-    all_res = [*res, far_res, across(far_res)]
-    back = [backward(all_res[2 + dc], saved[1][dc]) for dc in (0, 1)]
-    blocks = weight_grads(
-        [*row_blocks[0], *row_blocks[1]], all_res, sides(0, near_back) + sides(1, back)
-    )
+    term = weight_grads(row_blocks[0], res, sides(0, near_back), None)
+
+    res = [far_res, across(far_res)]
+    back = [backward(res[dc], saved[1][dc]) for dc in (0, 1)]
+    blocks = weight_grads(row_blocks[1], res, sides(1, back), term)
     got = x_stage(blocks)
     far_both = joined(back[0][2], back[1][2], rows)
     far_sum = scatter_y(far_both, far_both[0]).astype(BF)

time: 357 us -> 358 us (level)
  the two profiles are of different devices: /device:TPU:35 before, /device:TPU:38 now
where the time goes in v2:
time: 358 us; the launch traced here: 351 us
  waiting for transfers between devices  194 us (54%)
  starting transfers between devices  62.2 us (17%)
  matrix products  38.9 us (11%)
  Pallas kernels  24.1 us (7%)
  other arithmetic  20 us (6%)
  local copies, waits for them, and re-layouts  9.97 us (3%)
    ppermute x36, waiting for transfers between devices, from_expert(): return lax.ppermute(value, 'expert', expert_perm(dy, dz, dc))  154 us
    ppermute x36, starting transfers between devices, from_expert(): return lax.ppermute(value, 'expert', expert_perm(dy, dz, dc))  49.6 us
    dot_general x16, matrix products, mm(): return lax.dot_general(a, b, (dims, ((), ())), preferred_element_type=F32)  38.9 us
    ppermute x9, waiting for transfers between devices, from_dp(): return lax.ppermute(value, 'dp', dp_perm(dzl, dx))  37.8 us
    pallas_call x2, Pallas kernels, weight_grads(): pl.pallas_call(functools.partial(grad_kernel, first=acc is None), grid_sp...  24.1 us
    ppermute x9, starting transfers between devices, from_dp(): return lax.ppermute(value, 'dp', dp_perm(dzl, dx))  9 us
  transfers between devices with their start and end apart: 46, of which 29 were waited for; matrix products, arithmetic and copies ran while one was open for 13% of the time, Pallas kernels for 3%

profile of v2, /device:TPU:38, one launch (start us, length us, event | category | flops | bytes accessed | tf_op | source)
XLA Modules:
  0.0 351.3 jit_solution(6459460771689958537)
XLA Ops:
  5.3 6.3 %collective-permute-start.3 = (bf16[128,2048]{1,0:T(8,128)(2,1)}, bf16[128,2048]{1,0:T(8,128)(2,1)}, u32[]{:S(2)}, u32[]{:S(2)}) collective-permute-start(bf16[128,2048]{1,0:T(8,128)(2,1)} %param.7), channel_id=1, source_target_pairs={{2,0},{3,1},{0,2},{1,3},{6,4},{7,5},{4,6},{5,7},{10,8},{11,9},{8,1... | collective-permute-start | bytes 1572872 | tf_op jit(solution)/shard_map/ppermute | solution.py:38
  17.4 9.1 %collective-permute-done = bf16[128,2048]{1,0:T(8,128)(2,1)} collective-permute-done((bf16[128,2048]{1,0:T(8,128)(2,1)}, bf16[128,2048]{1,0:T(8,128)(2,1)}, u32[]{:S(2)}, u32[]{:S(2)}) %collective-permute-start) | collective-permute-done | bytes 524320 | tf_op jit(solution)/shard_map/ppermute | solution.py:38
  26.5 3.7 %collective-permute-done.2 = bf16[128,2048]{1,0:T(8,128)(2,1)} collective-permute-done((bf16[128,2048]{1,0:T(8,128)(2,1)}, bf16[128,2048]{1,0:T(8,128)(2,1)}, u32[]{:S(2)}, u32[]{:S(2)}) %collective-permute-start.2) | collective-permute-done | bytes 524320 | tf_op jit(solution)/shard_map/ppermute | solution.py:38
  36.6 4.1 %collective-permute-done.7.refs_1_ = bf16[512,2048]{1,0:T(8,128)(2,1)} collective-permute-done((bf16[512,2048]{1,0:T(8,128)(2,1)}, bf16[512,2048]{1,0:T(8,128)(2,1)}, u32[]{:S(2)}, u32[]{:S(2)}) %collective-permute-start.7) | collective-permute-done | bytes 2097184 | tf_op jit(solution)/shard_map/ppermute | solution.py:38
  53.8 18.8 %collective-permute-done.4 = bf16[128,2048]{1,0:T(8,128)(2,1)S(1)} collective-permute-done((bf16[128,2048]{1,0:T(8,128)(2,1)}, bf16[128,2048]{1,0:T(8,128)(2,1)S(1)}, u32[]{:S(2)}, u32[]{:S(2)}) %collective-permute-start.4) | collective-permute-done | bytes 524320 | tf_op jit(solution)/shard_map/ppermute | solution.py:38
  78.4 4.1 %collective-permute-done.12.refs_1_ = bf16[512,2048]{1,0:T(8,128)(2,1)S(1)} collective-permute-done((bf16[512,2048]{1,0:T(8,128)(2,1)S(1)}, bf16[512,2048]{1,0:T(8,128)(2,1)S(1)}, u32[]{:S(2)}, u32[]{:S(2)}) %collective-permute-start.12) | collective-permute-done | bytes 2097184 | tf_op jit(solution)/shard_map/ppermute | solution.py:38
  98.4 8.9 %collective-permute-done.14 = bf16[128,2048]{1,0:T(8,128)(2,1)S(1)} collective-permute-done((bf16[128,2048]{1,0:T(8,128)(2,1)S(1)}, bf16[128,2048]{1,0:T(8,128)(2,1)S(1)}, u32[]{:S(2)}, u32[]{:S(2)}) %collective-permute-start.14) | collective-permute-done | bytes 524320 | tf_op jit(solution)/shard_map/ppermute | solution.py:38
  107.9 9.8 %collective-permute-done.15 = bf16[128,2048]{1,0:T(8,128)(2,1)S(1)} collective-permute-done((bf16[128,2048]{1,0:T(8,128)(2,1)S(1)}, bf16[128,2048]{1,0:T(8,128)(2,1)S(1)}, u32[]{:S(2)}, u32[]{:S(2)}) %collective-permute-start.15) | collective-permute-done | bytes 524320 | tf_op jit(solution)/shard_map/ppermute | solution.py:38
  118.2 5.6 %collective-permute-start.17 = (bf16[128,2048]{1,0:T(8,128)(2,1)S(1)}, bf16[128,2048]{1,0:T(8,128)(2,1)S(1)}, u32[]{:S(2)}, u32[]{:S(2)}) collective-permute-start(bf16[128,2048]{1,0:T(8,128)(2,1)S(1)} %add_convert_fusion.10), channel_id=1, source_target_pairs={{2,0},{3,1},{0,2},{1,3},{6,4},{7,5},{4,6},{5,7},{10,8},{11,9},{8,1... | collective-permute-start | bytes 1572872 | tf_op jit(solution)/shard_map/ppermute | solution.py:38
  123.7 5.9 %collective-permute-done.10 = bf16[128,2048]{1,0:T(8,128)(2,1)S(1)} collective-permute-done((bf16[128,2048]{1,0:T(8,128)(2,1)S(1)}, bf16[128,2048]{1,0:T(8,128)(2,1)S(1)}, u32[]{:S(2)}, u32[]{:S(2)}) %collective-permute-start.10) | collective-permute-done | bytes 524320 | tf_op jit(solution)/shard_map/ppermute | solution.py:38
  129.7 10.5 %collective-permute-done.9 = bf16[128,2048]{1,0:T(8,128)(2,1)S(1)} collective-permute-done((bf16[128,2048]{1,0:T(8,128)(2,1)S(1)}, bf16[128,2048]{1,0:T(8,128)(2,1)S(1)}, u32[]{:S(2)}, u32[]{:S(2)}) %collective-permute-start.9) | collective-permute-done | bytes 524320 | tf_op jit(solution)/shard_map/ppermute | solution.py:38
  140.1 5.2 %collective-permute-done.17 = bf16[128,2048]{1,0:T(8,128)(2,1)S(1)} collective-permute-done((bf16[128,2048]{1,0:T(8,128)(2,1)S(1)}, bf16[128,2048]{1,0:T(8,128)(2,1)S(1)}, u32[]{:S(2)}, u32[]{:S(2)}) %collective-permute-start.17) | collective-permute-done | bytes 524320 | tf_op jit(solution)/shard_map/ppermute | solution.py:38
  148.8 4.6 %collective-permute-start.21 = (bf16[128,2048]{1,0:T(8,128)(2,1)S(1)}, bf16[128,2048]{1,0:T(8,128)(2,1)S(1)}, u32[]{:S(2)}, u32[]{:S(2)}) collective-permute-start(bf16[128,2048]{1,0:T(8,128)(2,1)S(1)} %get-tuple-element.59), channel_id=1, source_target_pairs={{2,0},{3,1},{0,2},{1,3},{6,4},{7,5},{4,6},{5,7},{10,8},{11,9},{8,1... | collective-permute-start | bytes 1572872 | tf_op jit(solution)/shard_map/ppermute | solution.py:38
  153.3 8.2 %collective-permute-done.18 = bf16[128,2048]{1,0:T(8,128)(2,1)S(1)} collective-permute-done((bf16[128,2048]{1,0:T(8,128)(2,1)S(1)}, bf16[128,2048]{1,0:T(8,128)(2,1)S(1)}, u32[]{:S(2)}, u32[]{:S(2)}) %collective-permute-start.18) | collective-permute-done | bytes 524320 | tf_op jit(solution)/shard_map/ppermute | solution.py:38
  163.9 10.0 %collective-permute-done.20 = bf16[128,2048]{1,0:T(8,128)(2,1)S(1)} collective-permute-done((bf16[128,2048]{1,0:T(8,128)(2,1)S(1)}, bf16[128,2048]{1,0:T(8,128)(2,1)S(1)}, u32[]{:S(2)}, u32[]{:S(2)}) %collective-permute-start.20) | collective-permute-done | bytes 524320 | tf_op jit(solution)/shard_map/ppermute | solution.py:38
  178.3 11.9 %collective-permute-done.27 = bf16[128,2048]{1,0:T(8,128)(2,1)S(1)} collective-permute-done((bf16[128,2048]{1,0:T(8,128)(2,1)S(1)}, bf16[128,2048]{1,0:T(8,128)(2,1)S(1)}, u32[]{:S(2)}, u32[]{:S(2)}) %collective-permute-start.27) | collective-permute-done | bytes 524320 | tf_op jit(solution)/shard_map/ppermute | solution.py:38
  193.2 8.8 %collective-permute-done.29 = bf16[128,2048]{1,0:T(8,128)(2,1)S(1)} collective-permute-done((bf16[128,2048]{1,0:T(8,128)(2,1)S(1)}, bf16[128,2048]{1,0:T(8,128)(2,1)S(1)}, u32[]{:S(2)}, u32[]{:S(2)}) %collective-permute-start.29) | collective-permute-done | bytes 524320 | tf_op jit(solution)/shard_map/ppermute | solution.py:38
  203.1 5.0 %multiply_convert_fusion.7 = (bf16[512,384]{1,0:T(8,128)(2,1)}, bf16[512,384]{1,0:T(8,128)(2,1)}) fusion(f32[512,768]{1,0:T(8,128)} %copy-done.9, bf16[512,2048]{1,0:T(8,128)(2,1)} %pad_maximum_fusion.2.refs_2_, bf16[1,384,2048]{2,1,0:T(8,128)(2,1)} %param.13, f32[512]{0:T(512)S(1)} %get-tuple-element.72), kind=kOutput, calls=%fused_computation.90 | convolution fusion | flops 808058880 | bytes 6031360 | tf_op jit(solution)/shard_map/dot_general | solution.py:46
  208.1 4.1 %multiply_convert_fusion.3 = (bf16[512,384]{1,0:T(8,128)(2,1)}, bf16[512,384]{1,0:T(8,128)(2,1)}) fusion(f32[512,768]{1,0:T(8,128)S(1)} %copy-done.12, bf16[512,2048]{1,0:T(8,128)(2,1)} %constant_dynamic-update-slice_fusion.refs_2_, bf16[1,384,2048]{2,1,0:T(8,128)(2,1)S(1)} %copy-done.27, f32[512]{0:T(512)S(1)} %get-tuple-element.74), kind=kOutput, calls=%fused_computation.86 | convolution fusion | flops 808058880 | bytes 6031360 | tf_op jit(solution)/shard_map/dot_general | solution.py:46
  212.2 4.0 %multiply_convert_fusion.5 = (bf16[512,384]{1,0:T(8,128)(2,1)}, bf16[512,384]{1,0:T(8,128)(2,1)}) fusion(f32[512,768]{1,0:T(8,128)S(1)} %copy-done.8, bf16[512,2048]{1,0:T(8,128)(2,1)} %collective-permute-done.22.refs_3_, bf16[1,384,2048]{2,1,0:T(8,128)(2,1)S(1)} %copy-done.27, f32[512]{0:T(512)S(1)} %get-tuple-element.73), kind=kOutput, calls=%fused_computation.88 | convolution fusion | flops 808058880 | bytes 6031360 | tf_op jit(solution)/shard_map/dot_general | solution.py:46
  216.2 11.4 %weight_grads.2.refs_10_ = f32[1152,2048]{1,0:T(8,128)} custom-call(s32[1]{0:T(128)} %bitcast.5.x_ref, bf16[512,2048]{1,0:T(8,128)(2,1)} %pad_maximum_fusion.refs_0_, bf16[512,2048]{1,0:T(8,128)(2,1)} %collective-permute-done.7.refs_1_, bf16[512,2048]{1,0:T(8,128)(2,1)} %pad_maximum_fusion.2.refs_2_, bf16[512,2048]{1,0:T(8,128)(2,1)} %collective-permute-done.22.refs_3_, ...), custom_call_target="tpu_custom_call" | custom-call | flops 4831838208 | bytes 22544384 | tf_op jit(solution)/shard_map/weight_grads/pallas_call | solution.py:123
  227.6 4.8 %multiply_convert_fusion.1 = (bf16[512,384]{1,0:T(8,128)(2,1)}, bf16[512,384]{1,0:T(8,128)(2,1)}) fusion(f32[512,768]{1,0:T(8,128)} %copy-done.10, bf16[512,2048]{1,0:T(8,128)(2,1)} %collective-permute-done.30.refs_3_, bf16[1,384,2048]{2,1,0:T(8,128)(2,1)} %param.13, f32[512]{0:T(512)S(1)} %get-tuple-element.75), kind=kOutput, calls=%fused_computation.84 | convolution fusion | flops 808058880 | bytes 6031360 | tf_op jit(solution)/shard_map/dot_general | solution.py:46
  232.4 12.7 %weight_grads.3 = bf16[4,4,1152,128]{3,2,1,0:T(8,128)(2,1)} custom-call(s32[1]{0:T(128)} %bitcast.5.x_ref, bf16[512,2048]{1,0:T(8,128)(2,1)} %copy-done.2, bf16[512,2048]{1,0:T(8,128)(2,1)} %copy-done.6, bf16[512,2048]{1,0:T(8,128)(2,1)} %constant_dynamic-update-slice_fusion.refs_2_, bf16[512,2048]{1,0:T(8,128)(2,1)} %collective-permute-done.30.refs_3_, ...), custom_call_target="tpu_custom_call" | custom-call | flops 4831838208 | bytes 22544384 | tf_op jit(solution)/shard_map/weight_grads/pallas_call | solution.py:123
  255.2 8.0 %collective-permute-done.36 = bf16[2,1152,128]{2,1,0:T(8,128)(2,1)S(1)} collective-permute-done((bf16[2,1152,128]{2,1,0:T(8,128)(2,1)S(1)}, bf16[2,1152,128]{2,1,0:T(8,128)(2,1)S(1)}, u32[]{:S(2)}, u32[]{:S(2)}) %collective-permute-start.36) | collective-permute-done | bytes 589856 | tf_op jit(solution)/shard_map/ppermute | solution.py:42
  265.5 10.3 %collective-permute-done.38 = bf16[2,1152,128]{2,1,0:T(8,128)(2,1)S(1)} collective-permute-done((bf16[2,1152,128]{2,1,0:T(8,128)(2,1)S(1)}, bf16[2,1152,128]{2,1,0:T(8,128)(2,1)S(1)}, u32[]{:S(2)}, u32[]{:S(2)}) %collective-permute-start.38) | collective-permute-done | bytes 589856 | tf_op jit(solution)/shard_map/ppermute | solution.py:42
  280.4 7.5 %collective-permute-done.37 = bf16[2,1152,128]{2,1,0:T(8,128)(2,1)S(1)} collective-permute-done((bf16[2,1152,128]{2,1,0:T(8,128)(2,1)S(1)}, bf16[2,1152,128]{2,1,0:T(8,128)(2,1)S(1)}, u32[]{:S(2)}, u32[]{:S(2)}) %collective-permute-start.37) | collective-permute-done | bytes 589856 | tf_op jit(solution)/shard_map/ppermute | solution.py:42
  300.7 8.0 %collective-permute-done.32 = bf16[128,2048]{1,0:T(8,128)(2,1)S(1)} collective-permute-done((bf16[128,2048]{1,0:T(8,128)(2,1)S(1)}, bf16[128,2048]{1,0:T(8,128)(2,1)S(1)}, u32[]{:S(2)}, u32[]{:S(2)}) %collective-permute-start.32) | collective-permute-done | bytes 524320 | tf_op jit(solution)/shard_map/ppermute | solution.py:38
  309.0 7.9 %collective-permute-done.33 = bf16[128,2048]{1,0:T(8,128)(2,1)S(1)} collective-permute-done((bf16[128,2048]{1,0:T(8,128)(2,1)S(1)}, bf16[128,2048]{1,0:T(8,128)(2,1)S(1)}, u32[]{:S(2)}, u32[]{:S(2)}) %collective-permute-start.33) | collective-permute-done | bytes 524320 | tf_op jit(solution)/shard_map/ppermute | solution.py:38
  321.9 4.5 %collective-permute-start.35 = (bf16[128,2048]{1,0:T(8,128)(2,1)}, bf16[128,2048]{1,0:T(8,128)(2,1)}, u32[]{:S(2)}, u32[]{:S(2)}) collective-permute-start(bf16[128,2048]{1,0:T(8,128)(2,1)} %add_convert_fusion.1), channel_id=1, source_target_pairs={{2,0},{3,1},{0,2},{1,3},{6,4},{7,5},{4,6},{5,7},{10,8},{11,9},{8,1... | collective-permute-start | bytes 1572872 | tf_op jit(solution)/shard_map/ppermute | solution.py:38
  326.4 7.1 %collective-permute-done.44 = bf16[1152,128]{1,0:T(8,128)(2,1)S(1)} collective-permute-done((bf16[1152,128]{1,0:T(8,128)(2,1)S(1)}, bf16[1152,128]{1,0:T(8,128)(2,1)S(1)}, u32[]{:S(2)}, u32[]{:S(2)}) %collective-permute-start.44) | collective-permute-done | bytes 294944 | tf_op jit(solution)/shard_map/ppermute | solution.py:42
  337.0 6.6 %collective-permute-done.25 = bf16[128,2048]{1,0:T(8,128)(2,1)} collective-permute-done((bf16[128,2048]{1,0:T(8,128)(2,1)}, bf16[128,2048]{1,0:T(8,128)(2,1)}, u32[]{:S(2)}, u32[]{:S(2)}) %collective-permute-start.25) | collective-permute-done | bytes 524320 | tf_op jit(solution)/shard_map/ppermute | solution.py:38
  343.6 4.1 %collective-permute-done.35 = bf16[128,2048]{1,0:T(8,128)(2,1)} collective-permute-done((bf16[128,2048]{1,0:T(8,128)(2,1)}, bf16[128,2048]{1,0:T(8,128)(2,1)}, u32[]{:S(2)}, u32[]{:S(2)}) %collective-permute-start.35) | collective-permute-done | bytes 524320 | tf_op jit(solution)/shard_map/ppermute | solution.py:38
  (187 shorter events, 108.2 us)
Async XLA Ops:
  0.6 25.9 %collective-permute-start = (bf16[128,2048]{1,0:T(8,128)(2,1)}, bf16[128,2048]{1,0:T(8,128)(2,1)}, u32[]{:S(2)}, u32[]{:S(2)}) collective-permute-start(bf16[128,2048]{1,0:T(8,128)(2,1)} %param.7), channel_id=1, source_target_pairs={{4,0},{5,1},{6,2},{7,3},{8,4},{9,5},{10,6},{11,7},{12,8},{13,9},{1... | collective-permute-start | bytes 1572872 | tf_op jit(solution)/shard_map/ppermute | solution.py:38
  3.7 22.8 %collective-permute-start.1 = (bf16[128,2048]{1,0:T(8,128)(2,1)}, bf16[128,2048]{1,0:T(8,128)(2,1)}, u32[]{:S(2)}, u32[]{:S(2)}) collective-permute-start(bf16[128,2048]{1,0:T(8,128)(2,1)} %param.7), channel_id=1, source_target_pairs={{8,0},{9,1},{10,2},{11,3},{12,4},{13,5},{14,6},{15,7},{0,8},{1,9},... | collective-permute-start | bytes 1572872 | tf_op jit(solution)/shard_map/ppermute | solution.py:38
  4.4 25.8 %collective-permute-start.2 = (bf16[128,2048]{1,0:T(8,128)(2,1)}, bf16[128,2048]{1,0:T(8,128)(2,1)}, u32[]{:S(2)}, u32[]{:S(2)}) collective-permute-start(bf16[128,2048]{1,0:T(8,128)(2,1)} %param.7), channel_id=1, source_target_pairs={{12,0},{13,1},{14,2},{15,3},{0,4},{1,5},{2,6},{3,7},{4,8},{5,9},{6... | collective-permute-start | bytes 1572872 | tf_op jit(solution)/shard_map/ppermute | solution.py:38
  5.3 30.9 %collective-permute-start.3 = (bf16[128,2048]{1,0:T(8,128)(2,1)}, bf16[128,2048]{1,0:T(8,128)(2,1)}, u32[]{:S(2)}, u32[]{:S(2)}) collective-permute-start(bf16[128,2048]{1,0:T(8,128)(2,1)} %param.7), channel_id=1, source_target_pairs={{2,0},{3,1},{0,2},{1,3},{6,4},{7,5},{4,6},{5,7},{10,8},{11,9},{8,1... | collective-permute-start | bytes 1572872 | tf_op jit(solution)/shard_map/ppermute | solution.py:38
  13.7 22.5 %all-to-all-start = ((f32[16,1,128]{2,1,0:T(1,128)}), f32[16,1,128]{2,1,0:T(1,128)S(1)}, u32[]{:S(2)}, u32[]{:S(2)}) async-start(f32[16,1,128]{2,1,0:T(1,128)} %bitcast.1), calls=%async_computation | async-start | bytes 16384 | tf_op jit(solution)/shard_map/all_to_all | solution.py:184
  46.8 30.7 %collective-permute-start.8 = (bf16[512,2048]{1,0:T(8,128)(2,1)S(1)}, bf16[512,2048]{1,0:T(8,128)(2,1)S(1)}, u32[]{:S(2)}, u32[]{:S(2)}) collective-permute-start(bf16[512,2048]{1,0:T(8,128)(2,1)S(1)} %convolution_convert_fusion.2), channel_id=1, source_target_pairs={{1,0},{0,1},{3,2},{2,3},{5,4},{4,5},{7,6},{6,7},{9,8},{8,9},{11,10... | collective-permute-start | bytes 6291464 | tf_op jit(solution)/shard_map/ppermute | solution.py:38
  47.1 25.6 %collective-permute-start.4 = (bf16[128,2048]{1,0:T(8,128)(2,1)}, bf16[128,2048]{1,0:T(8,128)(2,1)S(1)}, u32[]{:S(2)}, u32[]{:S(2)}) collective-permute-start(bf16[128,2048]{1,0:T(8,128)(2,1)} %collective-permute-done.3), channel_id=1, source_target_pairs={{4,0},{5,1},{6,2},{7,3},{8,4},{9,5},{10,6},{11,7},{12,8},{13,9},{1... | collective-permute-start | bytes 1572872 | tf_op jit(solution)/shard_map/ppermute | solution.py:38
  49.3 23.3 %collective-permute-start.5 = (bf16[128,2048]{1,0:T(8,128)(2,1)}, bf16[128,2048]{1,0:T(8,128)(2,1)S(1)}, u32[]{:S(2)}, u32[]{:S(2)}) collective-permute-start(bf16[128,2048]{1,0:T(8,128)(2,1)} %collective-permute-done.3), channel_id=1, source_target_pairs={{8,0},{9,1},{10,2},{11,3},{12,4},{13,5},{14,6},{15,7},{0,8},{1,9},... | collective-permute-start | bytes 1572872 | tf_op jit(solution)/shard_map/ppermute | solution.py:38
  49.9 26.2 %collective-permute-start.6 = (bf16[128,2048]{1,0:T(8,128)(2,1)}, bf16[128,2048]{1,0:T(8,128)(2,1)S(1)}, u32[]{:S(2)}, u32[]{:S(2)}) collective-permute-start(bf16[128,2048]{1,0:T(8,128)(2,1)} %collective-permute-done.3), channel_id=1, source_target_pairs={{12,0},{13,1},{14,2},{15,3},{0,4},{1,5},{2,6},{3,7},{4,8},{5,9},{6... | collective-permute-start | bytes 1572872 | tf_op jit(solution)/shard_map/ppermute | solution.py:38
  91.6 26.2 %collective-permute-start.15 = (bf16[128,2048]{1,0:T(8,128)(2,1)S(1)}, bf16[128,2048]{1,0:T(8,128)(2,1)S(1)}, u32[]{:S(2)}, u32[]{:S(2)}) collective-permute-start(bf16[128,2048]{1,0:T(8,128)(2,1)S(1)} %get-tuple-element.58), channel_id=1, source_target_pairs={{12,0},{13,1},{14,2},{15,3},{0,4},{1,5},{2,6},{3,7},{4,8},{5,9},{6... | collective-permute-start | bytes 1572872 | tf_op jit(solution)/shard_map/ppermute | solution.py:38
  92.4 25.3 %collective-permute-start.16 = (bf16[128,2048]{1,0:T(8,128)(2,1)S(1)}, bf16[128,2048]{1,0:T(8,128)(2,1)S(1)}, u32[]{:S(2)}, u32[]{:S(2)}) collective-permute-start(bf16[128,2048]{1,0:T(8,128)(2,1)S(1)} %get-tuple-element.57), channel_id=1, source_target_pairs={{4,0},{5,1},{6,2},{7,3},{8,4},{9,5},{10,6},{11,7},{12,8},{13,9},{1... | collective-permute-start | bytes 1572872 | tf_op jit(solution)/shard_map/ppermute | solution.py:38
  95.2 34.5 %collective-permute-start.10 = (bf16[128,2048]{1,0:T(8,128)(2,1)S(1)}, bf16[128,2048]{1,0:T(8,128)(2,1)S(1)}, u32[]{:S(2)}, u32[]{:S(2)}) collective-permute-start(bf16[128,2048]{1,0:T(8,128)(2,1)S(1)} %get-tuple-element.54), channel_id=1, source_target_pairs={{12,0},{13,1},{14,2},{15,3},{0,4},{1,5},{2,6},{3,7},{4,8},{5,9},{6... | collective-permute-start | bytes 1572872 | tf_op jit(solution)/shard_map/ppermute | solution.py:38
  95.2 34.5 %collective-permute-start.11 = (bf16[128,2048]{1,0:T(8,128)(2,1)S(1)}, bf16[128,2048]{1,0:T(8,128)(2,1)S(1)}, u32[]{:S(2)}, u32[]{:S(2)}) collective-permute-start(bf16[128,2048]{1,0:T(8,128)(2,1)S(1)} %get-tuple-element.53), channel_id=1, source_target_pairs={{4,0},{5,1},{6,2},{7,3},{8,4},{9,5},{10,6},{11,7},{12,8},{13,9},{1... | collective-permute-start | bytes 1572872 | tf_op jit(solution)/shard_map/ppermute | solution.py:38
  107.3 32.9 %collective-permute-start.9 = (bf16[128,2048]{1,0:T(8,128)(2,1)S(1)}, bf16[128,2048]{1,0:T(8,128)(2,1)S(1)}, u32[]{:S(2)}, u32[]{:S(2)}) collective-permute-start(bf16[128,2048]{1,0:T(8,128)(2,1)S(1)} %get-tuple-element.52), channel_id=1, source_target_pairs={{8,0},{9,1},{10,2},{11,3},{12,4},{13,5},{14,6},{15,7},{0,8},{1,9},... | collective-permute-start | bytes 1572872 | tf_op jit(solution)/shard_map/ppermute | solution.py:38
  118.2 27.2 %collective-permute-start.17 = (bf16[128,2048]{1,0:T(8,128)(2,1)S(1)}, bf16[128,2048]{1,0:T(8,128)(2,1)S(1)}, u32[]{:S(2)}, u32[]{:S(2)}) collective-permute-start(bf16[128,2048]{1,0:T(8,128)(2,1)S(1)} %add_convert_fusion.10), channel_id=1, source_target_pairs={{2,0},{3,1},{0,2},{1,3},{6,4},{7,5},{4,6},{5,7},{10,8},{11,9},{8,1... | collective-permute-start | bytes 1572872 | tf_op jit(solution)/shard_map/ppermute | solution.py:38
  147.9 25.9 %collective-permute-start.20 = (bf16[128,2048]{1,0:T(8,128)(2,1)S(1)}, bf16[128,2048]{1,0:T(8,128)(2,1)S(1)}, u32[]{:S(2)}, u32[]{:S(2)}) collective-permute-start(bf16[128,2048]{1,0:T(8,128)(2,1)S(1)} %get-tuple-element.59), channel_id=1, source_target_pairs={{12,0},{13,1},{14,2},{15,3},{0,4},{1,5},{2,6},{3,7},{4,8},{5,9},{6... | collective-permute-start | bytes 1572872 | tf_op jit(solution)/shard_map/ppermute | solution.py:38
  148.8 26.7 %collective-permute-start.21 = (bf16[128,2048]{1,0:T(8,128)(2,1)S(1)}, bf16[128,2048]{1,0:T(8,128)(2,1)S(1)}, u32[]{:S(2)}, u32[]{:S(2)}) collective-permute-start(bf16[128,2048]{1,0:T(8,128)(2,1)S(1)} %get-tuple-element.59), channel_id=1, source_target_pairs={{2,0},{3,1},{0,2},{1,3},{6,4},{7,5},{4,6},{5,7},{10,8},{11,9},{8,1... | collective-permute-start | bytes 1572872 | tf_op jit(solution)/shard_map/ppermute | solution.py:38
  176.4 25.6 %collective-permute-start.29 = (bf16[128,2048]{1,0:T(8,128)(2,1)S(1)}, bf16[128,2048]{1,0:T(8,128)(2,1)S(1)}, u32[]{:S(2)}, u32[]{:S(2)}) collective-permute-start(bf16[128,2048]{1,0:T(8,128)(2,1)S(1)} %collective-permute-done.21), channel_id=1, source_target_pairs={{12,0},{13,1},{14,2},{15,3},{0,4},{1,5},{2,6},{3,7},{4,8},{5,9},{6... | collective-permute-start | bytes 1572872 | tf_op jit(solution)/shard_map/ppermute | solution.py:38
  177.5 34.8 %collective-permute-start.22 = (bf16[512,2048]{1,0:T(8,128)(2,1)}, bf16[512,2048]{1,0:T(8,128)(2,1)}, u32[]{:S(2)}, u32[]{:S(2)}) collective-permute-start(bf16[512,2048]{1,0:T(8,128)(2,1)} %pad_maximum_fusion.2.refs_2_), channel_id=1, source_target_pairs={{1,0},{0,1},{3,2},{2,3},{5,4},{4,5},{7,6},{6,7},{9,8},{8,9},{11,10... | collective-permute-start | bytes 6291464 | tf_op jit(solution)/shard_map/ppermute | solution.py:38
  202.8 24.7 %collective-permute-start.30 = (bf16[512,2048]{1,0:T(8,128)(2,1)}, bf16[512,2048]{1,0:T(8,128)(2,1)}, u32[]{:S(2)}, u32[]{:S(2)}) collective-permute-start(bf16[512,2048]{1,0:T(8,128)(2,1)} %constant_dynamic-update-slice_fusion.refs_2_), channel_id=1, source_target_pairs={{1,0},{0,1},{3,2},{2,3},{5,4},{4,5},{7,6},{6,7},{9,8},{8,9},{11,10... | collective-permute-start | bytes 6291464 | tf_op jit(solution)/shard_map/ppermute | solution.py:38
  250.8 45.4 %collective-permute-start.23 = (bf16[512,2048]{1,0:T(8,128)(2,1)S(1)}, bf16[512,2048]{1,0:T(8,128)(2,1)S(1)}, u32[]{:S(2)}, u32[]{:S(2)}) collective-permute-start(bf16[512,2048]{1,0:T(8,128)(2,1)S(1)} %fusion.19), channel_id=1, source_target_pairs={{1,0},{0,1},{3,2},{2,3},{5,4},{4,5},{7,6},{6,7},{9,8},{8,9},{11,10... | collective-permute-start | bytes 6291464 | tf_op jit(solution)/shard_map/ppermute | solution.py:38
  251.0 24.9 %collective-permute-start.38 = (bf16[2,1152,128]{2,1,0:T(8,128)(2,1)S(1)}, bf16[2,1152,128]{2,1,0:T(8,128)(2,1)S(1)}, u32[]{:S(2)}, u32[]{:S(2)}) collective-permute-start(bf16[2,1152,128]{2,1,0:T(8,128)(2,1)S(1)} %get-tuple-element.45), channel_id=1, source_target_pairs={{48,0},{0,16},{16,32},{32,48},{112,64},{64,80},{80,96},{96,112},{1... | collective-permute-start | bytes 1769480 | tf_op jit(solution)/shard_map/ppermute | solution.py:42
  254.8 25.5 %collective-permute-start.39 = (bf16[2,1152,128]{2,1,0:T(8,128)(2,1)S(1)}, bf16[2,1152,128]{2,1,0:T(8,128)(2,1)S(1)}, u32[]{:S(2)}, u32[]{:S(2)}) collective-permute-start(bf16[2,1152,128]{2,1,0:T(8,128)(2,1)S(1)} %get-tuple-element.44), channel_id=1, source_target_pairs={{16,0},{32,16},{48,32},{0,48},{80,64},{96,80},{112,96},{64,112},{1... | collective-permute-start | bytes 1769480 | tf_op jit(solution)/shard_map/ppermute | solution.py:42
  263.2 28.5 %collective-permute-start.31 = (bf16[512,2048]{1,0:T(8,128)(2,1)S(1)}, bf16[512,2048]{1,0:T(8,128)(2,1)S(1)}, u32[]{:S(2)}, u32[]{:S(2)}) collective-permute-start(bf16[512,2048]{1,0:T(8,128)(2,1)S(1)} %fusion.25), channel_id=1, source_target_pairs={{1,0},{0,1},{3,2},{2,3},{5,4},{4,5},{7,6},{6,7},{9,8},{8,9},{11,10... | collective-permute-start | bytes 6291464 | tf_op jit(solution)/shard_map/ppermute | solution.py:38
  265.2 22.7 %collective-permute-start.37 = (bf16[2,1152,128]{2,1,0:T(8,128)(2,1)S(1)}, bf16[2,1152,128]{2,1,0:T(8,128)(2,1)S(1)}, u32[]{:S(2)}, u32[]{:S(2)}) collective-permute-start(bf16[2,1152,128]{2,1,0:T(8,128)(2,1)S(1)} %get-tuple-element.40), channel_id=1, source_target_pairs={{48,0},{0,16},{16,32},{32,48},{112,64},{64,80},{80,96},{96,112},{1... | collective-permute-start | bytes 1769480 | tf_op jit(solution)/shard_map/ppermute | solution.py:42
  292.8 24.1 %collective-permute-start.33 = (bf16[128,2048]{1,0:T(8,128)(2,1)S(1)}, bf16[128,2048]{1,0:T(8,128)(2,1)S(1)}, u32[]{:S(2)}, u32[]{:S(2)}) collective-permute-start(bf16[128,2048]{1,0:T(8,128)(2,1)S(1)} %get-tuple-element.51), channel_id=1, source_target_pairs={{12,0},{13,1},{14,2},{15,3},{0,4},{1,5},{2,6},{3,7},{4,8},{5,9},{6... | collective-permute-start | bytes 1572872 | tf_op jit(solution)/shard_map/ppermute | solution.py:38
  296.1 23.7 %collective-permute-start.42 = (bf16[1152,128]{1,0:T(8,128)(2,1)S(1)}, bf16[1152,128]{1,0:T(8,128)(2,1)S(1)}, u32[]{:S(2)}, u32[]{:S(2)}) collective-permute-start(bf16[1152,128]{1,0:T(8,128)(2,1)S(1)} %get-tuple-element.69), channel_id=1, source_target_pairs={{128,0},{144,16},{160,32},{176,48},{192,64},{208,80},{224,96},{240... | collective-permute-start | bytes 884744 | tf_op jit(solution)/shard_map/ppermute | solution.py:42
  296.2 25.7 %collective-permute-start.43 = (bf16[1152,128]{1,0:T(8,128)(2,1)S(1)}, bf16[1152,128]{1,0:T(8,128)(2,1)S(1)}, u32[]{:S(2)}, u32[]{:S(2)}) collective-permute-start(bf16[1152,128]{1,0:T(8,128)(2,1)S(1)} %get-tuple-element.71), channel_id=1, source_target_pairs={{192,0},{208,16},{224,32},{240,48},{0,64},{16,80},{32,96},{48,112}... | collective-permute-start | bytes 884744 | tf_op jit(solution)/shard_map/ppermute | solution.py:42
  308.7 24.8 %collective-permute-start.44 = (bf16[1152,128]{1,0:T(8,128)(2,1)S(1)}, bf16[1152,128]{1,0:T(8,128)(2,1)S(1)}, u32[]{:S(2)}, u32[]{:S(2)}) collective-permute-start(bf16[1152,128]{1,0:T(8,128)(2,1)S(1)} %get-tuple-element.70), channel_id=1, source_target_pairs={{64,0},{80,16},{96,32},{112,48},{128,64},{144,80},{160,96},{176,11... | collective-permute-start | bytes 884744 | tf_op jit(solution)/shard_map/ppermute | solution.py:42
  317.5 26.1 %collective-permute-start.25 = (bf16[128,2048]{1,0:T(8,128)(2,1)}, bf16[128,2048]{1,0:T(8,128)(2,1)}, u32[]{:S(2)}, u32[]{:S(2)}) collective-permute-start(bf16[128,2048]{1,0:T(8,128)(2,1)} %get-tuple-element.48), channel_id=1, source_target_pairs={{12,0},{13,1},{14,2},{15,3},{0,4},{1,5},{2,6},{3,7},{4,8},{5,9},{6... | collective-permute-start | bytes 1572872 | tf_op jit(solution)/shard_map/ppermute | solution.py:38
  319.8 23.8 %collective-permute-start.26 = (bf16[128,2048]{1,0:T(8,128)(2,1)}, bf16[128,2048]{1,0:T(8,128)(2,1)}, u32[]{:S(2)}, u32[]{:S(2)}) collective-permute-start(bf16[128,2048]{1,0:T(8,128)(2,1)} %get-tuple-element.47), channel_id=1, source_target_pairs={{4,0},{5,1},{6,2},{7,3},{8,4},{9,5},{10,6},{11,7},{12,8},{13,9},{1... | collective-permute-start | bytes 1572872 | tf_op jit(solution)/shard_map/ppermute | solution.py:38
  321.9 25.8 %collective-permute-start.35 = (bf16[128,2048]{1,0:T(8,128)(2,1)}, bf16[128,2048]{1,0:T(8,128)(2,1)}, u32[]{:S(2)}, u32[]{:S(2)}) collective-permute-start(bf16[128,2048]{1,0:T(8,128)(2,1)} %add_convert_fusion.1), channel_id=1, source_target_pairs={{2,0},{3,1},{0,2},{1,3},{6,4},{7,5},{4,6},{5,7},{10,8},{11,9},{8,1... | collective-permute-start | bytes 1572872 | tf_op jit(solution)/shard_map/ppermute | solution.py:38
  (44 other events, 465.4 us)
